TPU v7x, 128 devices: a whole 4x4x4 slice. The times are simulated.
128 devices in a mesh: band: 32 (over z, x, core), sector: 4 (over y).
Axes of the slice: x: 4, y: 4, z: 4, core: 2. Of those that a mesh axis runs over, the one named last changes fastest.
Arguments:
- node_latent: bfloat16 [65536, 256], P(('band', 'sector')), may hold values from -6 to 6
- edge_latent: bfloat16 [786432, 256], P(('band', 'sector')), may hold values from -6 to 6
- sender_slot: int32 [65536, 12], P(('band', 'sector')), may hold values from 0 to 1023, as said below
- edge_mask: int32 [65536, 12], P(('band', 'sector')), may hold values 0 or 1
- send_rows: int32 [128, 8, 64], P(('band', 'sector')), may hold values from 0 to 511
- w_edge_in: bfloat16 [768, 256], replicated, may hold values from -0.21875 to 0.21875
- b_edge: float32 [256], replicated, may hold values from -3 to 3
- w_edge_out: bfloat16 [256, 256], replicated, may hold values from -0.375 to 0.375
- g_edge: float32 [256], replicated, may hold values from 0.1 to 1.9
- w_node_in: bfloat16 [512, 256], replicated, may hold values from -0.25 to 0.25
- b_node: float32 [256], replicated, may hold values from -3 to 3
- w_node_out: bfloat16 [256, 256], replicated, may hold values from -0.375 to 0.375
- g_node: float32 [256], replicated, may hold values from 0.1 to 1.9
- node_cot: bfloat16 [65536, 256], P(('band', 'sector')), may hold values from -6 to 6
- edge_cot: bfloat16 [786432, 256], P(('band', 'sector')), may hold values from -6 to 6
Outputs:
- node_new: bfloat16 [65536, 256], P(('band', 'sector'))
- edge_new: bfloat16 [786432, 256], P(('band', 'sector'))
- node_grad: float32 [65536, 256], P(('band', 'sector'))
- edge_grad: bfloat16 [786432, 256], P(('band', 'sector'))
- grad_edge_in: float32 [768, 256], replicated
- grad_edge_out: float32 [256, 256], replicated
- grad_node_in: float32 [512, 256], replicated
- grad_node_out: float32 [256, 256], replicated
Inputs may be any that keep to these rules, and one draw needn't show every extreme that they name: `sender_slot`: values below 512 name the receiver owner's own nodes; value 512 + j * 64 + c names row send_rows[q, j, c] of the neighbouring owner q in direction j; directions that would leave the first or last band never occur.
All inputs are finite; a program needn't handle non-finite values. No bound on the sum of `edge_mask` on one device may be relied on, other than what follows from the above.
Results may differ from a plain program's by a relative error of at most 0.013.
Values may be sent and summed in bfloat16 or wider, within the bound.
A program may use at most 128 MiB of HBM per device.

v0:
```python
import jax
import jax.numpy as jnp
from jax import lax
from jax.sharding import PartitionSpec as P

band_steps = (-1, -1, -1, 0, 0, 1, 1, 1)
sector_steps = (-1, 0, 1, -1, 1, -1, 0, 1)


def passed_along(array, axis, by):
    count = lax.axis_size(axis)
    return lax.ppermute(array, axis, [(i, (i + by) % count) for i in range(count)])


def from_behind(array, axis, by):
    count = lax.axis_size(axis)
    pairs = [(i, i + by) for i in range(count) if 0 <= i + by < count]
    return lax.ppermute(array, axis, pairs)


def layer_norm(values, gain):
    average = jnp.mean(values, -1, keepdims=True)
    centred = values - average
    variance = jnp.mean(centred * centred, -1, keepdims=True)
    return centred * lax.rsqrt(variance + 1e-05) * gain


def interact(
    own_f,
    sender_f,
    edge_block,
    mask_f,
    w_edge_in,
    b_edge,
    w_edge_out,
    g_edge,
    w_node_in,
    b_node,
    w_node_out,
    g_node,
):
    latent_width = own_f.shape[1]
    node_count = own_f.shape[0]
    slot_count = sender_f.shape[0] // node_count
    own_rows = own_f.astype(jnp.bfloat16)
    sender = sender_f.astype(jnp.bfloat16)
    from_edge = jnp.dot(edge_block, w_edge_in[:latent_width], preferred_element_type=jnp.float32)
    from_sender = jnp.dot(
        sender, w_edge_in[latent_width : 2 * latent_width], preferred_element_type=jnp.float32
    )
    from_receiver = jnp.dot(
        own_rows, w_edge_in[2 * latent_width :], preferred_element_type=jnp.float32
    )
    pre_edge = (
        (from_edge + from_sender).reshape(node_count, slot_count, latent_width)
        + from_receiver[:, None, :]
        + b_edge
    )
    hidden = (
        jax.nn.silu(pre_edge).astype(jnp.bfloat16).reshape(node_count * slot_count, latent_width)
    )
    update = (
        layer_norm(jnp.dot(hidden, w_edge_out, preferred_element_type=jnp.float32), g_edge) * mask_f
    )
    edge_new = (edge_block.astype(jnp.float32) + update).astype(jnp.bfloat16)
    gathered = update.reshape(node_count, slot_count, latent_width).sum(1).astype(jnp.bfloat16)
    pre_node = jnp.dot(own_rows, w_node_in[:latent_width], preferred_element_type=jnp.float32)
    pre_node = (
        pre_node
        + jnp.dot(gathered, w_node_in[latent_width:], preferred_element_type=jnp.float32)
        + b_node
    )
    hidden_node = jax.nn.silu(pre_node).astype(jnp.bfloat16)
    node_new = (
        own_f
        + layer_norm(jnp.dot(hidden_node, w_node_out, preferred_element_type=jnp.float32), g_node)
    ).astype(jnp.bfloat16)
    return (node_new, edge_new)


def differentiate(own_f, sender_f, edge_block, mask_f, weights, node_cot, edge_cot):
    w_edge_in, b_edge, w_edge_out, g_edge, w_node_in, b_node, w_node_out, g_node = weights

    def local_layer(own_in, sender_in, edge_in, first_edge, second_edge, first_node, second_node):
        return interact(
            own_in,
            sender_in,
            edge_in,
            mask_f,
            first_edge,
            b_edge,
            second_edge,
            g_edge,
            first_node,
            b_node,
            second_node,
            g_node,
        )

    results, pullback = jax.vjp(
        local_layer, own_f, sender_f, edge_block, w_edge_in, w_edge_out, w_node_in, w_node_out
    )
    return (results, pullback((node_cot, edge_cot)))


def forward_pieces(pieces):
    arrived = []
    for course in range(8):
        moving = pieces[course]
        if sector_steps[course] != 0:
            moving = passed_along(moving, "sector", -sector_steps[course])
        if band_steps[course] != 0:
            moving = from_behind(moving, "band", -band_steps[course])
        arrived.append(moving)
    return jnp.stack(arrived)


def return_pieces(pieces):
    arrived = []
    for course in range(8):
        moving = pieces[course]
        if band_steps[course] != 0:
            moving = from_behind(moving.astype(jnp.bfloat16), "band", band_steps[course]).astype(
                moving.dtype
            )
        if sector_steps[course] != 0:
            moving = passed_along(
                moving.astype(jnp.bfloat16), "sector", sector_steps[course]
            ).astype(moving.dtype)
        arrived.append(moving)
    return jnp.stack(arrived)


def local(
    node_latent,
    edge_latent,
    sender_slot,
    edge_mask,
    send_rows,
    w_edge_in,
    b_edge,
    w_edge_out,
    g_edge,
    w_node_in,
    b_node,
    w_node_out,
    g_node,
    node_cot,
    edge_cot,
):
    node_count, latent_width = node_latent.shape
    slot_count = sender_slot.shape[1]
    capacity = send_rows.shape[2]
    device_count = lax.axis_size("band") * lax.axis_size("sector")
    requested = send_rows[0]
    outgoing = node_latent[requested]
    received = forward_pieces([outgoing[course] for course in range(8)]).reshape(
        8 * capacity, latent_width
    )
    node_f = node_latent.astype(jnp.float32)
    table_rows = jnp.concatenate([node_latent, received], axis=0)
    slot_flat = sender_slot.reshape(-1)
    table_count = node_count + 8 * capacity
    selector = (slot_flat[:, None] == jnp.arange(table_count, dtype=jnp.int32)[None, :]).astype(
        jnp.bfloat16
    )
    sender_f = jnp.dot(selector, table_rows, preferred_element_type=jnp.float32)
    mask_f = edge_mask.reshape(-1, 1).astype(jnp.float32)
    weights = (w_edge_in, b_edge, w_edge_out, g_edge, w_node_in, b_node, w_node_out, g_node)
    results, gradients = differentiate(
        node_f, sender_f, edge_latent, mask_f, weights, node_cot, edge_cot
    )
    d_own, d_sender, d_edge, g_first, g_second, g_third, g_fourth = gradients
    table_grad = lax.dot_general(
        selector,
        d_sender.astype(jnp.bfloat16),
        (((0,), (0,)), ((), ())),
        preferred_element_type=jnp.float32,
    )
    remote_grad = table_grad[node_count:].reshape(8, capacity, latent_width)
    arrived = return_pieces([remote_grad[course] for course in range(8)])
    node_grad = d_own + table_grad[:node_count]
    node_grad = node_grad.at[requested.reshape(-1)].add(arrived.reshape(-1, latent_width))
    summed = lax.psum(
        (
            g_first.astype(jnp.float32),
            g_second.astype(jnp.float32),
            g_third.astype(jnp.float32),
            g_fourth.astype(jnp.float32),
        ),
        ("band", "sector"),
    )
    grad_scale = float(device_count * node_count * slot_count) ** (-0.5)
    return (
        results[0],
        results[1],
        node_grad,
        d_edge,
        summed[0] * grad_scale,
        summed[1] * grad_scale,
        summed[2] * grad_scale,
        summed[3] * grad_scale,
    )


def solution(mesh):
    in_specs = (
        P(("band", "sector"), None),
        P(("band", "sector"), None),
        P(("band", "sector"), None),
        P(("band", "sector"), None),
        P(("band", "sector"), None, None),
        P(),
        P(),
        P(),
        P(),
        P(),
        P(),
        P(),
        P(),
        P(("band", "sector"), None),
        P(("band", "sector"), None),
    )
    out_specs = (
        P(("band", "sector"), None),
        P(("band", "sector"), None),
        P(("band", "sector"), None),
        P(("band", "sector"), None),
        P(),
        P(),
        P(),
        P(),
    )
    return jax.shard_map(local, mesh=mesh, in_specs=in_specs, out_specs=out_specs, check_vma=False)
```

profile of v0, /device:TPU:1, one launch (start us, length us, event | category | flops | bytes accessed | tf_op | source)
XLA Modules:
  0.0 368.5 jit_solution(13157726542673793157)
XLA Ops:
  8.0 2.5 gather_fusion
  10.6 2.2 collective-permute-start
  12.8 3.9 %collective-permute-start.2 = (bf16[64,256]{1,0:T(8,128)(2,1)S(1)}, bf16[64,256]{1,0:T(8,128)(2,1)S(1)}, u32[]{:S(2)}, u32[]{:S(2)}) collective-permute-start(bf16[64,256]{1,0:T(8,128)(2,1)S(1)} %get-tuple-element.50), channel_id=1, source_target_pairs={{0,4},{4,8},{8,12},{12,16},{16,20},{20,24},{24,28},{28,32},{32,36}... | collective-permute-start | bytes 98312 | tf_op jit(solution)/shard_map/ppermute | solution.py:18
  18.3 2.6 collective-permute-start.6
  22.1 5.5 %fusion.59 = f32[6144,256]{1,0:T(8,128)} fusion(bf16[6144,256]{1,0:T(8,128)(2,1)} %param.16, bf16[768,256]{1,0:T(8,128)(2,1)} %param.20), kind=kOutput, calls=%fused_computation.96 | convolution fusion | flops 805306368 | bytes 9568256 | tf_op jit(solution)/shard_map/jvp()/dot_general | solution.py:47
  27.9 2.8 collective-permute-start.1
  31.2 4.0 %add.138 = f32[512,12,256]{2,1,0:T(8,128)} broadcast(f32[512,256]{1,0:T(8,128)S(1)} %fusion.53), dimensions={0,2} | broadcast | bytes 6815744 | tf_op jit(solution)/shard_map/jvp()/add | solution.py:55
  35.2 8.7 %add.139 = f32[6144,256]{1,0:T(8,128)} reshape(f32[512,12,256]{2,1,0:T(8,128)} %add.138) | data formatting | bytes 12582912 | tf_op jit(solution)/shard_map/jvp()/add | solution.py:55
  44.5 2.7 collective-permute-start.10
  47.2 3.2 collective-permute-start.4
  50.5 1.9 collective-permute-start.9
  52.4 1.9 collective-permute-start.8
  54.3 2.1 collective-permute-start.11
  57.7 1.9 collective-permute-done.11
  59.6 5.1 %fusion.7 = bf16[6144,256]{1,0:T(8,128)(2,1)S(1)} fusion(s32[6144]{0:T(1024)S(1)} %eq.15, bf16[512,256]{1,0:T(8,128)(2,1)S(1)} %bitcast.86, bf16[512,256]{1,0:T(8,128)(2,1)S(1)} %copy-done.3), kind=kOutput, calls=%fused_computation.14 | convolution fusion | flops 3230138368 | bytes 3694592 | tf_op jit(solution)/shard_map/dot_general | solution.py:167
  64.8 5.0 %multiply_convert_fusion = (bf16[6144,256]{1,0:T(8,128)(2,1)S(1)}, f32[6144,256]{1,0:T(8,128)}) fusion(f32[256]{0:T(256)S(1)} %copy-done.39, f32[6144,256]{1,0:T(8,128)S(1)} %bitcast.82, f32[6144,256]{1,0:T(8,128)S(1)} %bitcast.80, bf16[6144,256]{1,0:T(8,128)(2,1)S(1)} %fusion.7, bf16[768,256]{1,0:T(8,128)(2,1)} %param.20), kind=kOutput, calls=%fused_computation.27 | convolution fusion | flops 817889280 | bytes 25297920 | tf_op jit(solution)/shard_map/jvp()/dot_general | solution.py:48
  71.5 1.9 multiply_reduce_fusion.1
  73.4 2.2 copy-done.10
  75.6 6.5 %add_convert_fusion = (bf16[6144,256]{1,0:T(8,128)(2,1)}, f32[6144,256]{1,0:T(8,128)}) fusion(bf16[6144,256]{1,0:T(8,128)(2,1)S(1)} %copy-done.10, f32[6144]{0:T(1024)S(1)} %convert_element_type.156, f32[256]{0:T(256)S(1)} %copy-done.36, f32[6144]{0:T(1024)S(1)} %fusion.64, f32[6144,256]{1,0:T(8,128)S(1)} %get-tuple-element.57, ...), kind=kLoop, calls=%fused_computation.24 | loop fusion | flops 11010048 | bytes 18949120 | tf_op jit(solution)/shard_map/jvp()/convert_element_type | solution.py:65
  82.1 8.4 %reshape.181 = f32[512,12,256]{2,1,0:T(8,128)} reshape(f32[6144,256]{1,0:T(8,128)} %get-tuple-element.33) | data formatting | bytes 12582912 | tf_op jit(solution)/shard_map/jvp()/reshape | solution.py:66
  90.5 5.0 %reduce_sum.91 = bf16[512,256]{1,0:T(8,128)(2,1)S(1)} reduce(f32[512,12,256]{2,1,0:T(8,128)} %reshape.181, f32[]{:T(128)} %constant.13.clone.1), dimensions={1}, to_apply=%region_2.3 | reduce | flops 1441792 | bytes 6553604 | tf_op jit(solution)/shard_map/jvp()/reduce_sum | solution.py:66
  101.1 4.0 %broadcast_in_dim.12 = f32[512,12,256]{2,1,0:T(8,128)} broadcast(f32[512,256]{1,0:T(8,128)S(1)} %fusion.18), dimensions={0,2} | broadcast | bytes 6815744 | tf_op jit(solution)/shard_map/transpose(jvp())/broadcast_in_dim | solution.py:66
  105.1 8.7 %reshape.182 = f32[6144,256]{1,0:T(8,128)} reshape(f32[512,12,256]{2,1,0:T(8,128)} %broadcast_in_dim.12) | data formatting | bytes 12582912 | tf_op jit(solution)/shard_map/transpose(jvp())/reshape | solution.py:66
  113.9 8.3 %multiply_reduce_fusion = f32[6144]{0:T(1024)S(1)} fusion(f32[6144,256]{1,0:T(8,128)} %copy-done.1, f32[6144,256]{1,0:T(8,128)} %reshape.182, bf16[6144,256]{1,0:T(8,128)(2,1)} %param.29, f32[6144]{0:T(1024)} %copy-done.22, f32[256]{0:T(256)S(1)} %copy-done.36, f32[6144]{0:T(1024)} %copy-done.17), kind=kLoop, calls=%fused_computation.22 | loop fusion | flops 11003904 | bytes 15803392 | tf_op jit(solution)/shard_map/transpose(jvp())/reduce_sum | solution.py:25
  123.5 6.7 %fusion.69 = (f32[6144]{0:T(1024)S(1)}, f32[6144,256]{1,0:T(8,128)S(1)}) fusion(f32[6144]{0:T(1024)S(1)} %multiply_multiply_fusion.2, f32[6144,256]{1,0:T(8,128)S(1)} %bitcast.78, f32[6144]{0:T(1024)S(1)} %copy-done.18, f32[6144]{0:T(1024)S(1)} %copy-done.26, f32[256]{0:T(256)S(1)} %copy-done.36, f32[6144]{0:T(1024)S(1)} %copy-done.23, ...), kind=kLoop, calls=%fused_computation.133 | loop fusion | flops 15722496 | bytes 22144000 | tf_op jit(solution)/shard_map/transpose(jvp())/reduce_sum | solution.py:23
  130.2 2.8 fusion.28
  133.1 8.7 %fusion.11 = (bf16[6144,256]{1,0:T(8,128)(2,1)}, f32[6144,256]{1,0:T(8,128)}) fusion(f32[256]{0:T(256)S(1)} %copy-done.39, f32[6144,256]{1,0:T(8,128)} %get-tuple-element.55, f32[6144,256]{1,0:T(8,128)S(1)} %bitcast.84, bf16[256,256]{1,0:T(8,128)(2,1)S(1)} %copy-done, f32[6144,256]{1,0:T(8,128)S(1)} %get-tuple-element.31, f32[6144]{0:T(1024)S(1)} %negate_multiply_fusion), kind=kOutput, calls=%fused_computation.21 | convolution fusion | flops 828899328 | bytes 28468224 | tf_op jit(solution)/shard_map/transpose(jvp())/dot_general | solution.py:63
  141.7 8.4 %reshape.183 = f32[512,12,256]{2,1,0:T(8,128)} reshape(f32[6144,256]{1,0:T(8,128)} %get-tuple-element.55) | data formatting | bytes 12582912 | tf_op jit(solution)/shard_map/jvp()/reshape | solution.py:55
  150.1 5.0 %fusion.77 = bf16[256,256]{0,1:T(8,128)(2,1)} fusion(bf16[6144,256]{1,0:T(8,128)(2,1)} %copy-done.41, bf16[6144,256]{1,0:T(8,128)(2,1)} %get-tuple-element.60), kind=kOutput, calls=%fused_computation.139 | convolution fusion | flops 805306368 | bytes 6422528 | tf_op jit(solution)/shard_map/transpose(jvp())/dot_general | solution.py:48
  155.1 1.7 fusion.33
  156.8 2.6 convolution_convert_fusion.1.clone.1.clone.5
  159.4 8.3 %reshape.186 = f32[512,12,256]{2,1,0:T(8,128)} reshape(f32[6144,256]{1,0:T(8,128)} %get-tuple-element.61) | data formatting | bytes 12582912 | tf_op jit(solution)/shard_map/transpose(jvp())/convert_element_type | solution.py:60
  167.7 8.7 %fusion.6 = bf16[512,256]{1,0:T(8,128)(2,1)S(1)} fusion(f32[512,12,256]{2,1,0:T(8,128)} %reshape.186, f32[512,12,256]{2,1,0:T(8,128)} %reshape.183, f32[256]{0:T(256)S(1)} %copy-done.39, f32[512,256]{1,0:T(8,128)S(1)} %fusion.53), kind=kLoop, calls=%fused_computation.12 | loop fusion | flops 18743296 | bytes 13370368 | tf_op jit(solution)/shard_map/transpose(jvp())/reduce_sum | solution.py:55
  177.0 2.7 fusion.9
  179.8 7.6 %fusion.74 = (bf16[1024,256]{1,0:T(8,128)(2,1)S(1)}, f32[1024,256]{1,0:T(8,128)S(1)}) fusion(s32[6144]{0:T(1024)S(1)} %copy-done.34, bf16[6144,256]{1,0:T(8,128)(2,1)S(1)} %copy-done.12), kind=kOutput, calls=%fused_computation.138 | convolution fusion | flops 3227779072 | bytes 4743168 | tf_op jit(solution)/shard_map/dot_general | solution.py:174
  187.4 2.1 collective-permute-start.12
  189.4 1.9 collective-permute-start.14
  191.4 1.9 collective-permute-start.15
  193.4 1.4 collective-permute-start.18
  199.6 5.1 %collective-permute-start.19 = (bf16[64,256]{1,0:T(8,128)(2,1)S(1)}, bf16[64,256]{1,0:T(8,128)(2,1)S(1)}, u32[]{:S(2)}, u32[]{:S(2)}) collective-permute-start(bf16[64,256]{1,0:T(8,128)(2,1)S(1)} %get-tuple-element.38), channel_id=1, source_target_pairs={{0,4},{4,8},{8,12},{12,16},{16,20},{20,24},{24,28},{28,32},{32,36}... | collective-permute-start | bytes 98312 | tf_op jit(solution)/shard_map/ppermute | solution.py:18
  204.7 1.9 collective-permute-start.22
  206.7 4.1 %collective-permute-start.21 = (bf16[64,256]{1,0:T(8,128)(2,1)S(1)}, bf16[64,256]{1,0:T(8,128)(2,1)S(1)}, u32[]{:S(2)}, u32[]{:S(2)}) collective-permute-start(bf16[64,256]{1,0:T(8,128)(2,1)S(1)} %get-tuple-element.37), channel_id=1, source_target_pairs={{0,4},{4,8},{8,12},{12,16},{16,20},{20,24},{24,28},{28,32},{32,36}... | collective-permute-start | bytes 98312 | tf_op jit(solution)/shard_map/ppermute | solution.py:18
  210.9 3.0 collective-permute-start.20
  214.9 3.2 collective-permute-done.23
  218.1 3.6 scatter_custom_fusion
  221.7 133.3 %all-reduce.8.cloned.1.call-done = (f32[768,256]{0,1:T(8,128)}, f32[256,256]{1,0:T(8,128)}, f32[512,256]{1,0:T(8,128)}, f32[256,256]{1,0:T(8,128)}) async-done(((f32[768,256]{0,1:T(8,128)}, f32[256,256]{1,0:T(8,128)}, f32[512,256]{1,0:T(8,128)}, f32[256,256]{1,0:T(8,128)}), (f32[768,256]{0,1:T(8,128)}, f32[256,256]{1,0:T(8,128)}, f32[512,256]{1,0:T(8,128)}, ...) | async-done | bytes 1835024 | tf_op jit(solution)/shard_map/psum | solution.py:184
  357.4 1.9 broadcast_multiply_fusion.1
  359.3 1.9 broadcast_multiply_fusion.2
  (194 shorter events, 23.4 us)
Async XLA Ops:
  7.2 62.6 %copy-start = (bf16[256,256]{1,0:T(8,128)(2,1)S(1)}, bf16[256,256]{1,0:T(8,128)(2,1)}, u32[]{:S(2)}) copy-start(bf16[256,256]{1,0:T(8,128)(2,1)} %param.22) | copy-start | bytes 393220
  7.2 347.8 %all-reduce.8.cloned.1.call-start = ((), (), s32[]{:S(2)}) async-start(), calls=%async_computation | async-start | bytes 3670016 | tf_op jit(solution)/shard_map/psum | solution.py:184
  10.6 17.3 %collective-permute-start = (bf16[64,256]{1,0:T(8,128)(2,1)S(1)}, bf16[64,256]{1,0:T(8,128)(2,1)S(1)}, u32[]{:S(2)}, u32[]{:S(2)}) collective-permute-start(bf16[64,256]{1,0:T(8,128)(2,1)S(1)} %get-tuple-element.51), channel_id=1, source_target_pairs={{0,1},{1,2},{2,3},{3,0},{4,5},{5,6},{6,7},{7,4},{8,9},{9,10},{10,1... | collective-permute-start | bytes 98312 | tf_op jit(solution)/shard_map/ppermute | solution.py:12
  12.8 31.7 %collective-permute-start.2 = (bf16[64,256]{1,0:T(8,128)(2,1)S(1)}, bf16[64,256]{1,0:T(8,128)(2,1)S(1)}, u32[]{:S(2)}, u32[]{:S(2)}) collective-permute-start(bf16[64,256]{1,0:T(8,128)(2,1)S(1)} %get-tuple-element.50), channel_id=1, source_target_pairs={{0,4},{4,8},{8,12},{12,16},{16,20},{20,24},{24,28},{28,32},{32,36}... | collective-permute-start | bytes 98312 | tf_op jit(solution)/shard_map/ppermute | solution.py:18
  16.8 30.5 %collective-permute-start.3 = (bf16[64,256]{1,0:T(8,128)(2,1)S(1)}, bf16[64,256]{1,0:T(8,128)(2,1)S(1)}, u32[]{:S(2)}, u32[]{:S(2)}) collective-permute-start(bf16[64,256]{1,0:T(8,128)(2,1)S(1)} %get-tuple-element.49), channel_id=1, source_target_pairs={{0,3},{1,0},{2,1},{3,2},{4,7},{5,4},{6,5},{7,6},{8,11},{9,8},{10,9... | collective-permute-start | bytes 98312 | tf_op jit(solution)/shard_map/ppermute | solution.py:12
  18.2 38.2 %collective-permute-start.5 = (bf16[64,256]{1,0:T(8,128)(2,1)S(1)}, bf16[64,256]{1,0:T(8,128)(2,1)S(1)}, u32[]{:S(2)}, u32[]{:S(2)}) collective-permute-start(bf16[64,256]{1,0:T(8,128)(2,1)S(1)} %get-tuple-element.48), channel_id=1, source_target_pairs={{0,1},{1,2},{2,3},{3,0},{4,5},{5,6},{6,7},{7,4},{8,9},{9,10},{10,1... | collective-permute-start | bytes 98312 | tf_op jit(solution)/shard_map/ppermute | solution.py:12
  18.3 9.3 %copy-start.3 = (bf16[512,256]{1,0:T(8,128)(2,1)S(1)}, bf16[512,256]{1,0:T(8,128)(2,1)}, u32[]{:S(2)}) copy-start(bf16[512,256]{1,0:T(8,128)(2,1)} %param.15) | copy-start | bytes 786436
  18.3 9.3 %copy-start.15 = (bf16[512,256]{1,0:T(8,128)(2,1)S(1)}, bf16[512,256]{1,0:T(8,128)(2,1)}, u32[]{:S(2)}) copy-start(bf16[512,256]{1,0:T(8,128)(2,1)} %param.24) | copy-start | bytes 786436
  18.3 38.2 %collective-permute-start.6 = (bf16[64,256]{1,0:T(8,128)(2,1)S(1)}, bf16[64,256]{1,0:T(8,128)(2,1)S(1)}, u32[]{:S(2)}, u32[]{:S(2)}) collective-permute-start(bf16[64,256]{1,0:T(8,128)(2,1)S(1)} %get-tuple-element.47), channel_id=1, source_target_pairs={{0,3},{1,0},{2,1},{3,2},{4,7},{5,4},{6,5},{7,6},{8,11},{9,8},{10,9... | collective-permute-start | bytes 98312 | tf_op jit(solution)/shard_map/ppermute | solution.py:12
  27.9 16.4 %collective-permute-start.1 = (bf16[64,256]{1,0:T(8,128)(2,1)S(1)}, bf16[64,256]{1,0:T(8,128)(2,1)S(1)}, u32[]{:S(2)}, u32[]{:S(2)}) collective-permute-start(bf16[64,256]{1,0:T(8,128)(2,1)S(1)} %collective-permute-done), channel_id=1, source_target_pairs={{0,4},{4,8},{8,12},{12,16},{16,20},{20,24},{24,28},{28,32},{32,36}... | collective-permute-start | bytes 98312 | tf_op jit(solution)/shard_map/ppermute | solution.py:18
  31.2 28.4 %copy-start.33 = (s32[6144]{0:T(1024)}, s32[6144]{0:T(1024)S(1)}, u32[]{:S(2)}) copy-start(s32[6144]{0:T(1024)S(1)} %eq.15) | copy-start | bytes 73732
  44.2 29.2 %copy-start.22 = (f32[6144]{0:T(1024)}, f32[6144]{0:T(1024)S(1)}, u32[]{:S(2)}) copy-start(f32[6144]{0:T(1024)S(1)} %convert_element_type.156) | copy-start | bytes 73732
  44.4 6.1 %collective-permute-start.7 = (bf16[64,256]{1,0:T(8,128)(2,1)S(1)}, bf16[64,256]{1,0:T(8,128)(2,1)S(1)}, u32[]{:S(2)}, u32[]{:S(2)}) collective-permute-start(bf16[64,256]{1,0:T(8,128)(2,1)S(1)} %get-tuple-element.46), channel_id=1, source_target_pairs={{0,1},{1,2},{2,3},{3,0},{4,5},{5,6},{6,7},{7,4},{8,9},{9,10},{10,1... | collective-permute-start | bytes 98312 | tf_op jit(solution)/shard_map/ppermute | solution.py:12
  44.5 20.2 %slice-start.2 = ((s8[6291456]{0:T(1024)(128)(4,1)}), s8[4194304]{0:T(1024)(128)(4,1)S(1)}, s32[]{:S(2)}) async-start(s8[6291456]{0:T(1024)(128)(4,1)} %bitcast.79), calls=%async_computation.3 | async-start | bytes 8388608
  44.5 7.9 %collective-permute-start.10 = (bf16[64,256]{1,0:T(8,128)(2,1)S(1)}, bf16[64,256]{1,0:T(8,128)(2,1)S(1)}, u32[]{:S(2)}, u32[]{:S(2)}) collective-permute-start(bf16[64,256]{1,0:T(8,128)(2,1)S(1)} %get-tuple-element.44), channel_id=1, source_target_pairs={{0,3},{1,0},{2,1},{3,2},{4,7},{5,4},{6,5},{7,6},{8,11},{9,8},{10,9... | collective-permute-start | bytes 98312 | tf_op jit(solution)/shard_map/ppermute | solution.py:12
  47.2 7.1 %collective-permute-start.4 = (bf16[64,256]{1,0:T(8,128)(2,1)S(1)}, bf16[64,256]{1,0:T(8,128)(2,1)S(1)}, u32[]{:S(2)}, u32[]{:S(2)}) collective-permute-start(bf16[64,256]{1,0:T(8,128)(2,1)S(1)} %collective-permute-done.3), channel_id=1, source_target_pairs={{0,4},{4,8},{8,12},{12,16},{16,20},{20,24},{24,28},{28,32},{32,36}... | collective-permute-start | bytes 98312 | tf_op jit(solution)/shard_map/ppermute | solution.py:18
  50.5 7.2 %collective-permute-start.9 = (bf16[64,256]{1,0:T(8,128)(2,1)S(1)}, bf16[64,256]{1,0:T(8,128)(2,1)S(1)}, u32[]{:S(2)}, u32[]{:S(2)}) collective-permute-start(bf16[64,256]{1,0:T(8,128)(2,1)S(1)} %get-tuple-element.45), channel_id=1, source_target_pairs={{4,0},{8,4},{12,8},{16,12},{20,16},{24,20},{28,24},{32,28},{36,32}... | collective-permute-start | bytes 98312 | tf_op jit(solution)/shard_map/ppermute | solution.py:18
  52.4 5.2 %collective-permute-start.8 = (bf16[64,256]{1,0:T(8,128)(2,1)S(1)}, bf16[64,256]{1,0:T(8,128)(2,1)S(1)}, u32[]{:S(2)}, u32[]{:S(2)}) collective-permute-start(bf16[64,256]{1,0:T(8,128)(2,1)S(1)} %collective-permute-done.7), channel_id=1, source_target_pairs={{4,0},{8,4},{12,8},{16,12},{20,16},{24,20},{28,24},{32,28},{36,32}... | collective-permute-start | bytes 98312 | tf_op jit(solution)/shard_map/ppermute | solution.py:18
  54.3 5.2 %collective-permute-start.11 = (bf16[64,256]{1,0:T(8,128)(2,1)S(1)}, bf16[64,256]{1,0:T(8,128)(2,1)S(1)}, u32[]{:S(2)}, u32[]{:S(2)}) collective-permute-start(bf16[64,256]{1,0:T(8,128)(2,1)S(1)} %collective-permute-done.10), channel_id=1, source_target_pairs={{4,0},{8,4},{12,8},{16,12},{20,16},{24,20},{28,24},{32,28},{36,32}... | collective-permute-start | bytes 98312 | tf_op jit(solution)/shard_map/ppermute | solution.py:18
  71.5 10.7 %copy-start.1 = (f32[6144,256]{1,0:T(8,128)}, f32[6144,256]{1,0:T(8,128)S(1)}, u32[]{:S(2)}) copy-start(f32[6144,256]{1,0:T(8,128)S(1)} %get-tuple-element.57) | copy-start | bytes 18874372
  71.5 10.6 %copy-start.17 = (f32[6144]{0:T(1024)}, f32[6144]{0:T(1024)S(1)}, u32[]{:S(2)}) copy-start(f32[6144]{0:T(1024)S(1)} %broadcast_multiply_fusion.4) | copy-start | bytes 73732
  105.1 17.2 %slice-start = ((s8[6291456]{0:T(1024)(128)(4,1)}), s8[2097152]{0:T(1024)(128)(4,1)S(1)}, s32[]{:S(2)}) async-start(s8[6291456]{0:T(1024)(128)(4,1)} %bitcast.77), calls=%async_computation.1 | async-start | bytes 4194304
  113.8 9.6 %copy-start.4 = (bf16[6144,256]{1,0:T(8,128)(2,1)S(1)}, bf16[6144,256]{1,0:T(8,128)(2,1)}, u32[]{:S(2)}) copy-start(bf16[6144,256]{1,0:T(8,128)(2,1)} %param.29) | copy-start | bytes 9437188
  113.8 9.6 %copy-start.18 = (f32[6144]{0:T(1024)S(1)}, f32[6144]{0:T(1024)}, u32[]{:S(2)}) copy-start(f32[6144]{0:T(1024)} %copy-done.17) | copy-start | bytes 73732
  113.8 9.6 %copy-start.23 = (f32[6144]{0:T(1024)S(1)}, f32[6144]{0:T(1024)}, u32[]{:S(2)}) copy-start(f32[6144]{0:T(1024)} %copy-done.22) | copy-start | bytes 73732
  113.9 9.6 %copy-start.26 = (f32[6144]{0:T(1024)S(1)}, f32[6144]{0:T(1024)}, u32[]{:S(2)}) copy-start(f32[6144]{0:T(1024)} %copy-done.25) | copy-start | bytes 73732
  122.2 10.9 %slice-start.6 = ((s8[6291456]{0:T(1024)(128)(4,1)}), s8[4194304]{0:T(1024)(128)(4,1)S(1)}, s32[]{:S(2)}) async-start(s8[6291456]{0:T(1024)(128)(4,1)} %bitcast.83), calls=%async_computation.7 | async-start | bytes 8388608
  123.5 9.6 %slice-start.7 = ((s8[6291456]{0:T(1024)(128)(4,1)}), s8[2097152]{0:T(1024)(128)(4,1)S(1)}, s32[]{:S(2)}) async-start(s8[6291456]{0:T(1024)(128)(4,1)} %bitcast.83), calls=%async_computation.8 | async-start | bytes 4194304
  167.7 9.3 %copy-start.7 = (bf16[6144,256]{1,0:T(8,128)(2,1)S(1)}, bf16[6144,256]{1,0:T(8,128)(2,1)}, u32[]{:S(2)}) copy-start(bf16[6144,256]{1,0:T(8,128)(2,1)} %get-tuple-element.60) | copy-start | bytes 9437188
  179.7 15.4 %copy-start.16 = (bf16[512,256]{1,0:T(8,128)(2,1)S(1)}, bf16[512,256]{1,0:T(8,128)(2,1)}, u32[]{:S(2)}) copy-start(bf16[512,256]{1,0:T(8,128)(2,1)} %param.24) | copy-start | bytes 786436
  179.7 15.7 %copy-start.29 = (bf16[256,256]{0,1:T(8,128)(2,1)S(1)}, bf16[256,256]{0,1:T(8,128)(2,1)}, u32[]{:S(2)}) copy-start(bf16[256,256]{0,1:T(8,128)(2,1)} %fusion.77) | copy-start | bytes 393220
  179.7 15.7 %copy-start.30 = (bf16[256,256]{0,1:T(8,128)(2,1)S(1)}, bf16[256,256]{0,1:T(8,128)(2,1)}, u32[]{:S(2)}) copy-start(bf16[256,256]{0,1:T(8,128)(2,1)} %fusion.33) | copy-start | bytes 393220
  179.7 17.9 %copy-start.20 = (bf16[256,256]{1,0:T(8,128)(2,1)S(1)}, bf16[256,256]{1,0:T(8,128)(2,1)}, u32[]{:S(2)}) copy-start(bf16[256,256]{1,0:T(8,128)(2,1)} %fusion.78) | copy-start | bytes 393220
  179.8 17.9 %copy-start.21 = (bf16[256,256]{1,0:T(8,128)(2,1)S(1)}, bf16[256,256]{1,0:T(8,128)(2,1)}, u32[]{:S(2)}) copy-start(bf16[256,256]{1,0:T(8,128)(2,1)} %fusion.32) | copy-start | bytes 393220
  187.3 11.3 %copy-start.14 = (bf16[512,256]{0,1:T(8,128)(2,1)S(1)}, bf16[512,256]{0,1:T(8,128)(2,1)}, u32[]{:S(2)}) copy-start(bf16[512,256]{0,1:T(8,128)(2,1)} %get-tuple-element.35) | copy-start | bytes 786436
  187.4 8.9 %collective-permute-start.12 = (bf16[64,256]{1,0:T(8,128)(2,1)S(1)}, bf16[64,256]{1,0:T(8,128)(2,1)}, u32[]{:S(2)}, u32[]{:S(2)}) collective-permute-start(bf16[64,256]{1,0:T(8,128)(2,1)S(1)} %get-tuple-element.43), channel_id=1, source_target_pairs={{4,0},{8,4},{12,8},{16,12},{20,16},{24,20},{28,24},{32,28},{36,32}... | collective-permute-start | bytes 98312 | tf_op jit(solution)/shard_map/ppermute | solution.py:18
  189.4 15.2 %collective-permute-start.14 = (bf16[64,256]{1,0:T(8,128)(2,1)S(1)}, bf16[64,256]{1,0:T(8,128)(2,1)S(1)}, u32[]{:S(2)}, u32[]{:S(2)}) collective-permute-start(bf16[64,256]{1,0:T(8,128)(2,1)S(1)} %get-tuple-element.42), channel_id=1, source_target_pairs={{4,0},{8,4},{12,8},{16,12},{20,16},{24,20},{28,24},{32,28},{36,32}... | collective-permute-start | bytes 98312 | tf_op jit(solution)/shard_map/ppermute | solution.py:18
  191.4 15.2 %collective-permute-start.15 = (bf16[64,256]{1,0:T(8,128)(2,1)S(1)}, bf16[64,256]{1,0:T(8,128)(2,1)S(1)}, u32[]{:S(2)}, u32[]{:S(2)}) collective-permute-start(bf16[64,256]{1,0:T(8,128)(2,1)S(1)} %get-tuple-element.41), channel_id=1, source_target_pairs={{4,0},{8,4},{12,8},{16,12},{20,16},{24,20},{28,24},{32,28},{36,32}... | collective-permute-start | bytes 98312 | tf_op jit(solution)/shard_map/ppermute | solution.py:18
  193.3 20.9 %collective-permute-start.17 = (bf16[64,256]{1,0:T(8,128)(2,1)S(1)}, bf16[64,256]{1,0:T(8,128)(2,1)S(1)}, u32[]{:S(2)}, u32[]{:S(2)}) collective-permute-start(bf16[64,256]{1,0:T(8,128)(2,1)S(1)} %get-tuple-element.40), channel_id=1, source_target_pairs={{0,3},{1,0},{2,1},{3,2},{4,7},{5,4},{6,5},{7,6},{8,11},{9,8},{10,9... | collective-permute-start | bytes 98312 | tf_op jit(solution)/shard_map/ppermute | solution.py:12
  193.4 20.8 %collective-permute-start.18 = (bf16[64,256]{1,0:T(8,128)(2,1)S(1)}, bf16[64,256]{1,0:T(8,128)(2,1)S(1)}, u32[]{:S(2)}, u32[]{:S(2)}) collective-permute-start(bf16[64,256]{1,0:T(8,128)(2,1)S(1)} %get-tuple-element.39), channel_id=1, source_target_pairs={{0,1},{1,2},{2,3},{3,0},{4,5},{5,6},{6,7},{7,4},{8,9},{9,10},{10,1... | collective-permute-start | bytes 98312 | tf_op jit(solution)/shard_map/ppermute | solution.py:12
  196.3 3.2 collective-permute-start.13
  199.6 7.2 %collective-permute-start.19 = (bf16[64,256]{1,0:T(8,128)(2,1)S(1)}, bf16[64,256]{1,0:T(8,128)(2,1)S(1)}, u32[]{:S(2)}, u32[]{:S(2)}) collective-permute-start(bf16[64,256]{1,0:T(8,128)(2,1)S(1)} %get-tuple-element.38), channel_id=1, source_target_pairs={{0,4},{4,8},{8,12},{12,16},{16,20},{20,24},{24,28},{28,32},{32,36}... | collective-permute-start | bytes 98312 | tf_op jit(solution)/shard_map/ppermute | solution.py:18
  204.7 6.2 %collective-permute-start.22 = (bf16[64,256]{1,0:T(8,128)(2,1)S(1)}, bf16[64,256]{1,0:T(8,128)(2,1)S(1)}, u32[]{:S(2)}, u32[]{:S(2)}) collective-permute-start(bf16[64,256]{1,0:T(8,128)(2,1)S(1)} %get-tuple-element.36), channel_id=1, source_target_pairs={{0,4},{4,8},{8,12},{12,16},{16,20},{20,24},{24,28},{28,32},{32,36}... | collective-permute-start | bytes 98312 | tf_op jit(solution)/shard_map/ppermute | solution.py:18
  206.6 7.2 %collective-permute-start.16 = (bf16[64,256]{1,0:T(8,128)(2,1)S(1)}, bf16[64,256]{1,0:T(8,128)(2,1)S(1)}, u32[]{:S(2)}, u32[]{:S(2)}) collective-permute-start(bf16[64,256]{1,0:T(8,128)(2,1)S(1)} %collective-permute-done.15), channel_id=1, source_target_pairs={{0,1},{1,2},{2,3},{3,0},{4,5},{5,6},{6,7},{7,4},{8,9},{9,10},{10,1... | collective-permute-start | bytes 98312 | tf_op jit(solution)/shard_map/ppermute | solution.py:12
  206.7 8.2 %collective-permute-start.21 = (bf16[64,256]{1,0:T(8,128)(2,1)S(1)}, bf16[64,256]{1,0:T(8,128)(2,1)S(1)}, u32[]{:S(2)}, u32[]{:S(2)}) collective-permute-start(bf16[64,256]{1,0:T(8,128)(2,1)S(1)} %get-tuple-element.37), channel_id=1, source_target_pairs={{0,4},{4,8},{8,12},{12,16},{16,20},{20,24},{24,28},{28,32},{32,36}... | collective-permute-start | bytes 98312 | tf_op jit(solution)/shard_map/ppermute | solution.py:18
  210.9 4.0 %collective-permute-start.20 = (bf16[64,256]{1,0:T(8,128)(2,1)S(1)}, bf16[64,256]{1,0:T(8,128)(2,1)S(1)}, u32[]{:S(2)}, u32[]{:S(2)}) collective-permute-start(bf16[64,256]{1,0:T(8,128)(2,1)S(1)} %collective-permute-done.19), channel_id=1, source_target_pairs={{0,3},{1,0},{2,1},{3,2},{4,7},{5,4},{6,5},{7,6},{8,11},{9,8},{10,9... | collective-permute-start | bytes 98312 | tf_op jit(solution)/shard_map/ppermute | solution.py:12
  213.9 4.3 %collective-permute-start.23 = (bf16[64,256]{1,0:T(8,128)(2,1)S(1)}, bf16[64,256]{1,0:T(8,128)(2,1)S(1)}, u32[]{:S(2)}, u32[]{:S(2)}) collective-permute-start(bf16[64,256]{1,0:T(8,128)(2,1)S(1)} %collective-permute-done.22), channel_id=1, source_target_pairs={{0,1},{1,2},{2,3},{3,0},{4,5},{5,6},{6,7},{7,4},{8,9},{9,10},{10,1... | collective-permute-start | bytes 98312 | tf_op jit(solution)/shard_map/ppermute | solution.py:12
  221.7 139.4 %copy-start.19 = (f32[512,256]{1,0:T(8,128)}, f32[512,256]{1,0:T(8,128)S(1)}, u32[]{:S(2)}) copy-start(f32[512,256]{1,0:T(8,128)S(1)} %scatter_custom_fusion) | copy-start | bytes 1572868
  (27 other events, 165.5 us)
Sparse Core Ops, SparseCore 0:
  199.7 155.3 all-reduce.7
where the time goes:
time: 375 us; the launch traced here: 368 us
  waiting for transfers between devices  140 us (37%)
  local copies, waits for them, and re-layouts  60.8 us (16%)
  matrix products  54.3 us (14%)
  other arithmetic  49.3 us (13%)
  starting transfers between devices  48.2 us (13%)
  between operations  15.6 us (4%)
    psum x1, waiting for transfers between devices, local(): lax.psum((g_first.astype(jnp.float32), g_second.astype(jnp.float32), g_th...  133 us
    ppermute x12, starting transfers between devices, from_behind(): return lax.ppermute(array, axis, pairs)  32.9 us
    reshape x2, local copies, waits for them, and re-layouts, interact(): update.reshape(node_count, slot_count, latent_width).sum(1)  17.1 us
    ppermute x12, starting transfers between devices, passed_along(): lax.ppermute(array, axis, [(i, (i + by) % count) for i in range(count)])  15.3 us
    add x2, local copies, waits for them, and re-layouts, interact(): (from_edge + from_sender).reshape(node_count, slot_count, latent_width)  12.7 us
    dot_general x3, matrix products, interact(): jnp.dot(sender, w_edge_in[latent_width:2 * latent_width], preferred_eleme...  12.6 us
    dot_general x3, matrix products, interact(): jnp.dot(hidden, w_edge_out, preferred_element_type=jnp.float32)  12.6 us
    dot_general x3, matrix products, interact(): jnp.dot(edge_block, w_edge_in[:latent_width], preferred_element_type=jnp....  9.87 us
  transfers between devices with their start and end apart: 25, of which 5 were waited for; matrix products, arithmetic and copies ran while one was open for 7% of the time, Pallas kernels for 0%

commit v1 on v0

v1 whole, which is shorter than its diff:
```python
import functools
import jax
import jax.numpy as jnp
from jax import lax
from jax.experimental import pallas as pl
from jax.experimental.pallas import tpu as pltpu
from jax.sharding import PartitionSpec as P

F32, BF16 = jnp.float32, jnp.bfloat16
R = 64
D = 256


def dot(a, b):
    return jnp.dot(a, b, preferred_element_type=F32)


def dot_rows(a, b):
    return lax.dot_general(a, b, (((0,), (0,)), ((), ())), preferred_element_type=F32)


def silu_parts(pre):
    gate = 0.5 * jnp.tanh(0.5 * pre) + 0.5
    hidden = pre * gate
    return hidden, gate + hidden * (1.0 - gate)


def centred(matrix):
    return matrix - jnp.mean(matrix, 1, keepdims=True)


def flipped(matrix):
    return jnp.transpose(matrix.astype(F32)).astype(BF16)


def layer_kernel(
    tiles, slots,
    own_ref, far_ref, edge_ref, slot_ref, mask_ref,
    w_ein, b_e, w_eout, g_e, w_nin, b_n, w_nout, g_n, ncot_ref, ecot_ref,
    nnew_ref, enew_ref, egrad_ref, ngrad_ref, back_ref, grads_ref,
    x_ref, xt_ref, wcat_ref, weo_ref, weot_ref, wet_ref, recv_ref, parts_ref,
    sel_ref, selt_ref, hid_ref, dsil_ref, xh_ref, rm_ref, gath_ref, dgath_ref,
    acc_ref, gout_ref, gd_ref, down_ref, gnode_ref,
):
    t = pl.program_id(0)
    rows = R * slots
    n = own_ref.shape[0]
    table = n + far_ref.shape[0]
    seg = D + table

    @pl.when(t == 0)
    def _():
        e = lax.broadcasted_iota(jnp.int32, (rows, 128), 0)
        l = lax.broadcasted_iota(jnp.int32, (rows, 128), 1)
        r = jnp.where(l >= R, l - R, l)
        gap = e - slots * r
        inside = (gap >= 0) & (gap < slots)
        x_ref[:, seg : seg + 128] = jnp.where(inside, 1.0, 0.0).astype(BF16)
        ef = e.astype(F32)
        k = ef - slots * jnp.floor((ef + 0.5) * (1.0 / slots))
        lf = l.astype(F32)
        sel_ref[...] = jnp.where(lf == k, 32.0, 0.0) + jnp.where(lf == k + 12.0, 1.0, 0.0)
        e = lax.broadcasted_iota(jnp.int32, (R, rows), 1)
        r = lax.broadcasted_iota(jnp.int32, (R, rows), 0)
        gap = e - slots * r
        inside = (gap >= 0) & (gap < slots)
        xt_ref[seg : seg + R, :] = jnp.where(inside, 1.0, 0.0).astype(BF16)
        ef = lax.broadcasted_iota(jnp.int32, (32, rows), 1).astype(F32)
        lf = lax.broadcasted_iota(jnp.int32, (32, rows), 0).astype(F32)
        k = ef - slots * jnp.floor((ef + 0.5) * (1.0 / slots))
        selt_ref[...] = jnp.where(lf == k, 32.0, 0.0) + jnp.where(lf == k + 12.0, 1.0, 0.0)
        v = slot_ref[...] + 1024 * mask_ref[...]
        high = (v >> 5).astype(F32)
        low = (v & 31).astype(F32)
        parts_ref[...] = jnp.concatenate(
            [high, low, jnp.zeros((n, 128 - 2 * slots), F32)], axis=1
        ).astype(BF16)
        wcat_ref[0:D, :] = w_ein[0:D, :]
        wcat_ref[D : D + n, :] = dot(own_ref[...], w_ein[D : 2 * D, :]).astype(BF16)
        wcat_ref[D + n : seg, :] = dot(far_ref[...], w_ein[D : 2 * D, :]).astype(BF16)
        recv_ref[...] = dot(own_ref[...], w_ein[2 * D :, :]) + b_e[...]
        weo = centred(w_eout[...].astype(F32))
        weo_ref[...] = weo.astype(BF16)
        weot_ref[...] = jnp.transpose(weo).astype(BF16)
        wet_ref[...] = flipped(w_ein[0:D, :])
        acc_ref[...] = jnp.zeros_like(acc_ref)
        gout_ref[...] = jnp.zeros_like(gout_ref)

    @pl.when(t < tiles)
    def _():
        here = pl.ds(pl.multiple_of(t * rows, rows), rows)
        mine = pl.ds(pl.multiple_of(t * R, R), R)
        edges = edge_ref[...]
        x_ref[:, 0:D] = edges
        spread = dot(x_ref[:, seg : seg + R], parts_ref[mine, :])
        v = jnp.sum(spread * sel_ref[...], 1, keepdims=True)
        real = v >= 1024.0
        slot = jnp.where(real, v - 1024.0, v)
        lane = lax.broadcasted_iota(jnp.int32, (rows, D), 1).astype(F32).astype(BF16)
        for block in range(table // D):
            wanted = (slot - float(block * D)).astype(BF16)
            x_ref[:, D + block * D : 2 * D + block * D] = jnp.where(
                lane == wanted, jnp.ones((), BF16), jnp.zeros((), BF16)
            )
        recv = recv_ref[mine, :]
        high = recv.astype(BF16)
        wcat_ref[seg : seg + R, :] = high
        wcat_ref[seg + R : seg + 2 * R, :] = (recv - high.astype(F32)).astype(BF16)
        pre = dot(x_ref[...], wcat_ref[...])
        hidden, slope = silu_parts(pre)
        hidden = hidden.astype(BF16)
        hid_ref[here, :] = hidden
        dsil_ref[here, :] = slope.astype(BF16)
        c = dot(hidden, weo_ref[...])
        rstd = lax.rsqrt(jnp.mean(c * c, 1, keepdims=True) + 1e-05)
        normed = c * rstd
        keep = jnp.where(real, 1.0, 0.0)
        xh_ref[here, :] = normed.astype(BF16)
        rm_ref[here, :] = rstd * keep
        update = normed * g_e[...] * keep
        enew_ref[...] = (edges.astype(F32) + update).astype(BF16)
        gath_ref[mine, :] = dot(xt_ref[seg : seg + R, :], update.astype(BF16)).astype(BF16)

    @pl.when(t == tiles)
    def _():
        own = own_ref[...]
        gath = gath_ref[...]
        pre = dot(own, w_nin[0:D, :]) + dot(gath, w_nin[D:, :]) + b_n[...]
        hidden, slope = silu_parts(pre)
        hidden = hidden.astype(BF16)
        wno = centred(w_nout[...].astype(F32))
        c = dot(hidden, wno.astype(BF16))
        rstd = lax.rsqrt(jnp.mean(c * c, 1, keepdims=True) + 1e-05)
        normed = c * rstd
        nnew_ref[...] = (own.astype(F32) + normed * g_n[...]).astype(BF16)
        cot = ncot_ref[...].astype(F32)
        dx = cot * g_n[...]
        share = jnp.mean(dx * normed, 1, keepdims=True)
        dz = (rstd * (dx - normed * share)).astype(BF16)
        gnode_ref[2 * D : 3 * D, :] = centred(dot_rows(hidden, dz))
        dpre = (dot(dz, jnp.transpose(wno).astype(BF16)) * slope).astype(BF16)
        gnode_ref[0:D, :] = dot_rows(own, dpre)
        gnode_ref[D : 2 * D, :] = dot_rows(gath, dpre)
        down_ref[...] = cot + dot(dpre, flipped(w_nin[0:D, :]))
        dgath_ref[...] = dot(dpre, flipped(w_nin[D:, :])).astype(BF16)

    @pl.when(t > tiles)
    def _():
        u = t - tiles - 1
        here = pl.ds(pl.multiple_of(u * rows, rows), rows)
        mine = pl.ds(pl.multiple_of(u * R, R), R)
        cot = ecot_ref[...].astype(F32)
        spread = dot(x_ref[:, seg : seg + R], dgath_ref[mine, :])
        dx = (cot + spread) * g_e[...]
        normed = xh_ref[here, :].astype(F32)
        share = jnp.mean(dx * normed, 1, keepdims=True)
        dz = (rm_ref[here, :] * (dx - normed * share)).astype(BF16)
        gout_ref[...] += dot_rows(hid_ref[here, :], dz)
        dpre = (dot(dz, weot_ref[...]) * dsil_ref[here, :].astype(F32)).astype(BF16)
        egrad_ref[...] = (cot + dot(dpre, wet_ref[...])).astype(BF16)
        part = dot_rows(parts_ref[mine, 0:32], xt_ref[seg : seg + R, :])
        v = jnp.sum(part * selt_ref[...], 0, keepdims=True)
        slot = jnp.where(v >= 1024.0, v - 1024.0, v)
        xt_ref[0:D, :] = jnp.transpose(edge_ref[...])
        line = lax.broadcasted_iota(jnp.int32, (D, rows), 0).astype(F32).astype(BF16)
        for block in range(table // D):
            wanted = (slot - float(block * D)).astype(BF16)
            xt_ref[D + block * D : 2 * D + block * D, :] = jnp.where(
                line == wanted, jnp.ones((), BF16), jnp.zeros((), BF16)
            )
        acc_ref[...] += dot(xt_ref[0:seg, :], dpre)
        gd_ref[mine, :] = dot(xt_ref[seg : seg + R, :], dpre).astype(BF16)

    @pl.when(t == 2 * tiles)
    def _():
        own = own_ref[...]
        near = acc_ref[D : D + n, :].astype(BF16)
        far = acc_ref[D + n : seg, :].astype(BF16)
        wst = flipped(w_ein[D : 2 * D, :])
        back_ref[...] = dot(far, wst).astype(BF16).reshape(back_ref.shape)
        gd = gd_ref[...]
        ngrad_ref[...] = down_ref[...] + dot(near, wst) + dot(gd, flipped(w_ein[2 * D :, :]))
        g_s = dot_rows(own, near) + dot_rows(far_ref[...], far)
        g_r = dot_rows(own, gd)
        whole = [acc_ref[0:D, :], g_s, g_r, centred(gout_ref[...])]
        whole += [gnode_ref[i * D : (i + 1) * D, :] for i in range(3)]
        at = 0
        for piece in whole:
            for i in range(D // 16):
                for j in range(2):
                    grads_ref[at] = piece[16 * i : 16 * i + 16, 128 * j : 128 * j + 128].astype(BF16)
                    at += 1


def layer_call(node, far, edge, slot, mask, w_ein, b_e, w_eout, g_e, w_nin, b_n, w_nout, g_n, ncot, ecot):
    n, d = node.shape
    slots = slot.shape[1]
    rows = R * slots
    tiles = n // R
    table = n + far.shape[0]
    seg = d + table
    total = n * slots
    whole = pl.BlockSpec(memory_space=pltpu.VMEM)
    stream_e = pl.BlockSpec((rows, d), lambda t: (jnp.where(t < tiles, t, jnp.maximum(t - tiles - 1, 0)), 0))
    first = pl.BlockSpec((rows, d), lambda t: (jnp.minimum(t, tiles - 1), 0))
    second = pl.BlockSpec((rows, d), lambda t: (jnp.maximum(t - tiles - 1, 0), 0))
    tiles_all = 7 * (d // 16) * (d // 128)
    flops = 2 * total * d * (d * 8 + 2 * table)
    return pl.pallas_call(
        functools.partial(layer_kernel, tiles, slots),
        grid=(2 * tiles + 1,),
        in_specs=[whole, whole, stream_e] + [whole] * 11 + [second],
        out_specs=[whole, first, second, whole, whole, whole],
        out_shape=[
            jax.ShapeDtypeStruct((n, d), BF16),
            jax.ShapeDtypeStruct((total, d), BF16),
            jax.ShapeDtypeStruct((total, d), BF16),
            jax.ShapeDtypeStruct((n, d), F32),
            jax.ShapeDtypeStruct((8, far.shape[0] // 8, d), BF16),
            jax.ShapeDtypeStruct((tiles_all, 16, 128), BF16),
        ],
        scratch_shapes=[
            pltpu.VMEM((rows, seg + 2 * R), BF16),
            pltpu.VMEM((seg + R, rows), BF16),
            pltpu.VMEM((seg + 2 * R, d), BF16),
            pltpu.VMEM((d, d), BF16),
            pltpu.VMEM((d, d), BF16),
            pltpu.VMEM((d, d), BF16),
            pltpu.VMEM((n, d), F32),
            pltpu.VMEM((n, 128), BF16),
            pltpu.VMEM((rows, 128), F32),
            pltpu.VMEM((32, rows), F32),
            pltpu.VMEM((total, d), BF16),
            pltpu.VMEM((total, d), BF16),
            pltpu.VMEM((total, d), BF16),
            pltpu.VMEM((total, 1), F32),
            pltpu.VMEM((n, d), BF16),
            pltpu.VMEM((n, d), BF16),
            pltpu.VMEM((seg, d), F32),
            pltpu.VMEM((d, d), F32),
            pltpu.VMEM((n, d), BF16),
            pltpu.VMEM((n, d), F32),
            pltpu.VMEM((3 * d, d), F32),
        ],
        compiler_params=pltpu.CompilerParams(vmem_limit_bytes=56 * 1024 * 1024),
        cost_estimate=pl.CostEstimate(flops=flops, bytes_accessed=5 * total * d * 2, transcendentals=total * d),
    )(node, far, edge, slot, mask, w_ein, b_e.reshape(1, -1), w_eout, g_e.reshape(1, -1), w_nin, b_n.reshape(1, -1), w_nout, g_n.reshape(1, -1), ncot, ecot)

band_steps = (-1, -1, -1, 0, 0, 1, 1, 1)
sector_steps = (-1, 0, 1, -1, 1, -1, 0, 1)
MESH = pl.DeviceIdType.MESH


def neighbours(bands, sectors):
    band, sector = lax.axis_index("band"), lax.axis_index("sector")
    ahead = [
        (lax.rem(band + b + bands, bands), lax.rem(sector + s + sectors, sectors))
        for b, s in zip(band_steps, sector_steps)
    ]
    return ahead


def greet(places):
    barrier = pltpu.get_barrier_semaphore()
    for place in places:
        pl.semaphore_signal(barrier, inc=1, device_id=place, device_id_type=MESH)
    pl.semaphore_wait(barrier, len(places))


def picked(wanted, count):
    line = lax.broadcasted_iota(jnp.int32, (count, wanted.shape[1]), 0)
    return jnp.where(line == wanted, 1.0, 0.0).astype(BF16)


def fetch_kernel(bands, sectors, node_ref, rows_ref, far_ref, out_ref, send_sem, recv_sem):
    ahead = neighbours(bands, sectors)
    barrier = pltpu.get_barrier_semaphore()
    for place in ahead:
        pl.semaphore_signal(barrier, inc=1, device_id=place, device_id_type=MESH)
    node = node_ref[...]
    for j in range(8):
        choice = picked(rows_ref[0, j : j + 1, :], node.shape[0])
        out_ref[j] = dot_rows(choice, node).astype(BF16)
    pl.semaphore_wait(barrier, 8)
    copies = []
    for j in range(8):
        copies.append(
            pltpu.make_async_remote_copy(
                src_ref=out_ref.at[j],
                dst_ref=far_ref.at[j],
                send_sem=send_sem.at[j],
                recv_sem=recv_sem.at[j],
                device_id=ahead[7 - j],
                device_id_type=MESH,
            )
        )
        copies[-1].start()
    for copy in copies:
        copy.wait()


def fetch_call(bands, sectors, node, rows):
    cap, d = rows.shape[2], node.shape[1]
    whole = pl.BlockSpec(memory_space=pltpu.VMEM)
    return pl.pallas_call(
        functools.partial(fetch_kernel, bands, sectors),
        in_specs=[whole, whole],
        out_specs=whole,
        out_shape=jax.ShapeDtypeStruct((8, cap, d), BF16),
        scratch_shapes=[
            pltpu.VMEM((8, cap, d), BF16),
            pltpu.SemaphoreType.DMA((8,)),
            pltpu.SemaphoreType.DMA((8,)),
        ],
        compiler_params=pltpu.CompilerParams(collective_id=0, has_side_effects=True),
    )(node, rows)


def sum_kernel(
    bands, sectors, share, back_ref, grads_ref, arrived_ref, out_ref,
    half_ref, one_ref, two_ref, three_ref, first_in, second_in, third_in,
    send_sem, recv_sem, core_sem, back_send, back_recv,
):
    ahead = neighbours(bands, sectors)
    band, sector = lax.axis_index("band"), lax.axis_index("sector")
    core = lax.rem(band, 2)
    x = lax.rem(band // 2, 4)
    z = band // 8
    at = {"x": x, "y": sector, "z": z}

    def place(axis, index):
        if axis == "x":
            return ((z * 4 + index) * 2 + core, sector)
        if axis == "z":
            return ((index * 4 + x) * 2 + core, sector)
        return (band, index)

    def others(axis):
        return [lax.rem(at[axis] + i, 4) for i in (1, 2, 3)]

    sibling = (band + 1 - 2 * core, sector)
    peers = [place("x", i) for i in others("x")] + [place("z", i) for i in others("z")]
    peers += [place("y", lax.rem(sector + 2, 4))]
    greet(ahead + peers)

    returns = []
    core_copy = pltpu.make_async_remote_copy(
        src_ref=grads_ref.at[1 - core], dst_ref=half_ref,
        send_sem=core_sem.at[0], recv_sem=core_sem.at[1],
        device_id=sibling, device_id_type=MESH,
    )
    core_copy.start()
    for j in range(8):
        returns.append(
            pltpu.make_async_remote_copy(
                src_ref=back_ref.at[j], dst_ref=arrived_ref.at[j],
                send_sem=back_send.at[j], recv_sem=back_recv.at[j],
                device_id=ahead[j], device_id_type=MESH,
            )
        )
        returns[-1].start()

    orders = (("x", "y", "z"), ("y", "z", "x"), ("z", "x", "y"))
    starts = [16 * sum(share[:p]) for p in range(3)]

    def exchange(stage, p, axis, source, target):
        copies = []
        for i, other in enumerate(others(axis)):
            copies.append(
                pltpu.make_async_remote_copy(
                    src_ref=source(other, i), dst_ref=target(i),
                    send_sem=send_sem.at[stage, p, i], recv_sem=recv_sem.at[stage, p, i],
                    device_id=place(axis, other), device_id_type=MESH,
                )
            )
            copies[-1].start()
        return copies

    def finish(copies):
        for copy in copies:
            copy.wait()

    core_copy.wait()
    one_ref[...] = (grads_ref[core].astype(F32) + half_ref[...].astype(F32)).astype(BF16)

    live = []
    for p in range(3):
        m, axis = share[p], orders[p][0]
        live.append(exchange(
            0, p, axis,
            lambda other, i, p=p, m=m: one_ref.at[pl.ds(starts[p] + other * (4 * m), 4 * m)],
            lambda i, p=p, m=m: first_in.at[i, pl.ds(4 * sum(share[:p]), 4 * m)],
        ))
    for p in range(3):
        m, axis, low = share[p], orders[p][0], 4 * sum(share[:p])
        finish(live[p])
        total = one_ref[pl.ds(starts[p] + at[axis] * (4 * m), 4 * m)].astype(F32)
        for i in range(3):
            total += first_in[i, low : low + 4 * m].astype(F32)
        two_ref[low : low + 4 * m] = total.astype(BF16)
        live[p] = exchange(
            1, p, orders[p][1],
            lambda other, i, low=low, m=m: two_ref.at[pl.ds(low + other * m, m)],
            lambda i, p=p, m=m: second_in.at[i, pl.ds(sum(share[:p]), m)],
        )
    for p in range(3):
        m, axis, low, mid = share[p], orders[p][1], sum(share[:p]), 4 * sum(share[:p])
        finish(live[p])
        total = two_ref[pl.ds(mid + at[axis] * m, m)].astype(F32)
        for i in range(3):
            total += second_in[i, low : low + m].astype(F32)
        three_ref[low : low + m] = total.astype(BF16)
        third = orders[p][2]
        third_in[at[third], low : low + m] = total.astype(BF16)
        live[p] = exchange(
            2, p, third,
            lambda other, i, low=low, m=m: three_ref.at[pl.ds(low, m)],
            lambda i, low=low, m=m, third=third: third_in.at[at[third], pl.ds(low, m)],
        )
    for p in range(3):
        m, low = share[p], sum(share[:p])
        finish(live[p])
        total = third_in[0, low : low + m].astype(F32)
        for i in range(1, 4):
            total += third_in[i, low : low + m].astype(F32)
        spot = starts[p] + at[orders[p][0]] * (4 * m) + at[orders[p][1]] * m
        out_ref[core, pl.ds(spot, m)] = total.astype(BF16)
        live[p] = exchange(
            3, p, orders[p][1],
            lambda other, i, spot=spot, m=m: out_ref.at[core, pl.ds(spot, m)],
            lambda i, spot=spot, m=m: out_ref.at[core, pl.ds(spot, m)],
        )
    for p in range(3):
        m = share[p]
        finish(live[p])
        spot = starts[p] + at[orders[p][0]] * (4 * m)
        live[p] = exchange(
            4, p, orders[p][0],
            lambda other, i, spot=spot, m=m: out_ref.at[core, pl.ds(spot, 4 * m)],
            lambda i, spot=spot, m=m: out_ref.at[core, pl.ds(spot, 4 * m)],
        )
    last = []
    for p in range(3):
        finish(live[p])
        spot, m = starts[p], 16 * share[p]
        last.append(pltpu.make_async_remote_copy(
            src_ref=out_ref.at[core, pl.ds(spot, m)], dst_ref=out_ref.at[core, pl.ds(spot, m)],
            send_sem=core_sem.at[2 + p], recv_sem=core_sem.at[5 + p],
            device_id=sibling, device_id_type=MESH,
        ))
        last[-1].start()
    finish(returns)
    finish(last)


def sum_call(bands, sectors, back, grads):
    half = grads.shape[0] // 2
    unit = half // 16
    share = (unit - 2 * (unit // 3), unit // 3, unit // 3)
    whole = pl.BlockSpec(memory_space=pltpu.VMEM)
    tile = grads.shape[1:]
    return pl.pallas_call(
        functools.partial(sum_kernel, bands, sectors, share),
        in_specs=[whole, whole],
        out_specs=[whole, whole],
        out_shape=[
            jax.ShapeDtypeStruct(back.shape, BF16),
            jax.ShapeDtypeStruct((2, half) + tile, BF16),
        ],
        scratch_shapes=[
            pltpu.VMEM((half,) + tile, BF16),
            pltpu.VMEM((half,) + tile, BF16),
            pltpu.VMEM((half // 4,) + tile, BF16),
            pltpu.VMEM((unit,) + tile, BF16),
            pltpu.VMEM((3, half // 4) + tile, BF16),
            pltpu.VMEM((3, unit) + tile, BF16),
            pltpu.VMEM((4, unit) + tile, BF16),
            pltpu.SemaphoreType.DMA((5, 3, 3)),
            pltpu.SemaphoreType.DMA((5, 3, 3)),
            pltpu.SemaphoreType.DMA((8,)),
            pltpu.SemaphoreType.DMA((8,)),
            pltpu.SemaphoreType.DMA((8,)),
        ],
        compiler_params=pltpu.CompilerParams(collective_id=1, has_side_effects=True),
    )(back, grads.reshape((2, half) + tile))


def close_kernel(scale, rows_ref, arrived_ref, part_ref, sums_ref, ngrad_ref, *outs):
    n = part_ref.shape[0]
    total = part_ref[...]
    for j in range(8):
        total += dot(picked(rows_ref[0, j : j + 1, :], n), arrived_ref[j])
    ngrad_ref[...] = total
    at = 0
    for out in outs:
        for i in range(out.shape[0] // 16):
            for j in range(out.shape[1] // 128):
                out[16 * i : 16 * i + 16, 128 * j : 128 * j + 128] = sums_ref[at].astype(F32) * scale
                at += 1


def close_call(scale, rows, arrived, part, sums):
    d = part.shape[1]
    whole = pl.BlockSpec(memory_space=pltpu.VMEM)
    outs = [part.shape, (3 * d, d), (d, d), (2 * d, d), (d, d)]
    return pl.pallas_call(
        functools.partial(close_kernel, scale),
        in_specs=[whole] * 4,
        out_specs=[whole] * 5,
        out_shape=[jax.ShapeDtypeStruct(shape, F32) for shape in outs],
        compiler_params=pltpu.CompilerParams(vmem_limit_bytes=32 * 1024 * 1024),
    )(rows, arrived, part, sums.reshape((-1,) + sums.shape[2:]))


def solution(mesh):
    bands, sectors = mesh.shape["band"], mesh.shape["sector"]

    def local(node, edge, slot, mask, rows, w_ein, b_e, w_eout, g_e, w_nin, b_n, w_nout, g_n, ncot, ecot):
        n, d = node.shape
        far = fetch_call(bands, sectors, node, rows)
        nnew, enew, egrad, part, back, grads = layer_call(
            node, far.reshape(-1, d), edge, slot, mask,
            w_ein, b_e, w_eout, g_e, w_nin, b_n, w_nout, g_n, ncot, ecot,
        )
        arrived, sums = sum_call(bands, sectors, back, grads)
        scale = float(bands * sectors * n * slot.shape[1]) ** (-0.5)
        outs = close_call(scale, rows, arrived, part, sums)
        return (nnew, enew, outs[0], egrad) + tuple(outs[1:])

    split = P(("band", "sector"), None)
    in_specs = (split,) * 4 + (P(("band", "sector"), None, None),) + (P(),) * 8 + (split, split)
    out_specs = (split,) * 4 + (P(),) * 4
    return jax.shard_map(local, mesh=mesh, in_specs=in_specs, out_specs=out_specs, check_vma=False)
```

time: 375 us -> 91.1 us (0.24); the launches traced: 368 us -> 90.6 us
  waiting for transfers between devices: 140 us -> 0 us
  Pallas kernels: 0 us -> 83.6 us
  local copies, waits for them, and re-layouts: 60.8 us -> 6.38 us
  matrix products: 54.3 us -> 0 us
  other arithmetic: 49.3 us -> 0 us
  starting transfers between devices: 48.2 us -> 0 us
  between operations: 15.6 us -> 0.68 us
    psum x1 -> x0, waiting for transfers between devices: 133 us -> none  [local(): lax.psum((g_first.astype(jnp.float32), g_second.astype(jnp.float32), g_th...]
    pallas_call x0 -> x4, Pallas kernels: none -> 83.6 us  [the longest x1 35.2 us: layer_call(): pl.pallas_call(functools.partial(layer_kernel, tiles, slots), grid=(2 * t...]
    dot_general x23 -> x0, matrix products: 54.3 us -> none  [the longest x3 12.6 us: interact(): jnp.dot(sender, w_edge_in[latent_width:2 * latent_width], preferred_eleme...]
    ppermute x24 -> x0, starting transfers between devices: 48.2 us -> none  [the longest x12 32.9 us: from_behind(): return lax.ppermute(array, axis, pairs)]
    reduce_sum x7 -> x0, other arithmetic: 31.7 us -> none  [the longest x1 8.72 us: interact(): (from_edge + from_sender).reshape(node_count, slot_count, latent_width)]
    reshape x3 -> x0, local copies, waits for them, and re-layouts: 25.5 us -> none  [the longest x2 17.1 us: interact(): update.reshape(node_count, slot_count, latent_width).sum(1)]
    add x3 -> x0, local copies, waits for them, and re-layouts: 12.8 us -> none  [the longest x2 12.7 us: interact(): (from_edge + from_sender).reshape(node_count, slot_count, latent_width)]
    convert_element_type x3 -> x0, local copies, waits for them, and re-layouts: 8.61 us -> none  [the longest x1 8.3 us: interact(): jax.nn.silu(pre_edge).astype(jnp.bfloat16)]
  transfers between devices with their start and end apart: 25 -> 0, of which waited for: 5 -> 0; matrix products, arithmetic and copies ran while one was open for 7% -> 0% of each run, Pallas kernels for 0% -> 0%
where the time goes in v1:
time: 91.1 us; the launch traced here: 90.6 us
  Pallas kernels  83.6 us (92%)
  local copies, waits for them, and re-layouts  6.38 us (7%)
    pallas_call x1, Pallas kernels, layer_call(): pl.pallas_call(functools.partial(layer_kernel, tiles, slots), grid=(2 * t...  35.2 us
    pallas_call x1, Pallas kernels, sum_call(): pl.pallas_call(functools.partial(sum_kernel, bands, sectors, share), in_s...  32.6 us
    pallas_call x1, Pallas kernels, fetch_call(): pl.pallas_call(functools.partial(fetch_kernel, bands, sectors), in_specs=...  13.7 us
    unnamed x10, local copies, waits for them, and re-layouts  6.38 us
    pallas_call x1, Pallas kernels, close_call(): pl.pallas_call(functools.partial(close_kernel, scale), in_specs=[whole] *...  2.08 us

profile of v1, /device:TPU:1, one launch (start us, length us, event | category | flops | bytes accessed | tf_op | source)
XLA Modules:
  0.0 90.6 jit_solution(3332779122960946580)
XLA Ops:
  0.6 1.6 %copy.23.slot_ref = s32[512,12]{1,0:T(8,128)} copy(s32[512,12]{0,1:T(8,128)} %param.17) | data formatting | bytes 49152 | tf_op args[2]
  2.2 1.6 %copy.24.mask_ref = s32[512,12]{1,0:T(8,128)} copy(s32[512,12]{0,1:T(8,128)} %param.18) | data formatting | bytes 49152 | tf_op args[3]
  3.8 13.7 %shard_map.206 = bf16[8,64,256]{2,1,0:T(8,128)(2,1)} custom-call(bf16[512,256]{1,0:T(8,128)(2,1)} %own_ref.1, s32[1,8,64]{2,1,0:T(8,128)} %rows_ref.3), custom_call_target="tpu_custom_call" | custom-call | tf_op jit(solution)/shard_map/pallas_call | solution.py:305
  17.6 0.0 copy-start.3
  17.6 35.2 %shard_map.207 = (bf16[512,256]{1,0:T(8,128)(2,1)}, bf16[6144,256]{1,0:T(8,128)(2,1)}, bf16[6144,256]{1,0:T(8,128)(2,1)}, f32[512,256]{1,0:T(8,128)}, bf16[8,64,...) custom-call(bf16[512,256]{1,0:T(8,128)(2,1)} %own_ref.1, bf16[512,256]{1,0:T(8,128)(2,1)} %bitcast.9, ...), custom_call_target="tpu_custom_call" | custom-call | flops 12884901888 | bytes 15728640 | tf_op jit(solution)/shard_map/pallas_call | solution.py:209
  52.7 32.6 %shard_map.208 = (bf16[8,64,256]{2,1,0:T(8,128)(2,1)}, bf16[2,112,16,128]{3,2,1,0:T(8,128)(2,1)}) custom-call(bf16[8,64,256]{2,1,0:T(8,128)(2,1)} %get-tuple-element.23.back_ref, bf16[2,112,16,128]{3,2,1,0:T(8,128)(2,1)} %bitcast.8), custom_call_target="tpu_custom_call" | custom-call | tf_op jit(solution)/shard_map/pallas_call | solution.py:462
  85.4 0.0 copy-done.3
  85.4 0.0 copy-start
  85.4 1.2 %copy-done = bf16[2,112,16,128]{3,2,1,0:T(8,128)(2,1)S(1)} copy-done((bf16[2,112,16,128]{3,2,1,0:T(8,128)(2,1)S(1)}, bf16[2,112,16,128]{3,2,1,0:T(8,128)(2,1)}, u32[]{:S(2)}) %copy-start) | copy-done | bytes 917528
  86.6 0.0 copy-start.1
  86.6 1.0 %copy-done.1 = f32[512,256]{1,0:T(8,128)S(1)} copy-done((f32[512,256]{1,0:T(8,128)S(1)}, f32[512,256]{1,0:T(8,128)}, u32[]{:S(2)}) %copy-start.1) | copy-done | bytes 524312
  87.6 0.0 copy-start.2
  87.6 0.9 %copy-done.2 = bf16[8,64,256]{2,1,0:T(8,128)(2,1)S(1)} copy-done((bf16[8,64,256]{2,1,0:T(8,128)(2,1)S(1)}, bf16[8,64,256]{2,1,0:T(8,128)(2,1)}, u32[]{:S(2)}) %copy-start.2) | copy-done | bytes 262168
  88.5 2.1 %shard_map.209 = (f32[512,256]{1,0:T(8,128)}, f32[768,256]{1,0:T(8,128)}, f32[256,256]{1,0:T(8,128)}, f32[512,256]{1,0:T(8,128)}, f32[256,256]{1,0:T(8,128)}) custom-call(s32[1,8,64]{2,1,0:T(8,128)S(1)} %copy-done.3, bf16[8,64,256]{2,1,0:T(8,128)(2,1)S(1)} %copy-done.2, f32[512,256]{1,0:T(8,128)S(1)} %copy-done.1, bf16[224,16,128]{2,1,0:T(8,128)(2,1)S(1)} %bitcast.7), custom_call_target="tpu_custom_call" | custom-call | tf_op jit(solution)/shard_map/pallas_call | solution.py:506
Async XLA Ops:
  17.6 67.8 %copy-start.3 = (s32[1,8,64]{2,1,0:T(8,128)S(1)}, s32[1,8,64]{2,1,0:T(8,128)}, u32[]{:S(2)}) copy-start(s32[1,8,64]{2,1,0:T(8,128)} %rows_ref.3) | copy-start | bytes 6148
  85.4 1.2 %copy-start = (bf16[2,112,16,128]{3,2,1,0:T(8,128)(2,1)S(1)}, bf16[2,112,16,128]{3,2,1,0:T(8,128)(2,1)}, u32[]{:S(2)}) copy-start(bf16[2,112,16,128]{3,2,1,0:T(8,128)(2,1)} %get-tuple-element.27) | copy-start | bytes 2752516
  86.6 1.0 %copy-start.1 = (f32[512,256]{1,0:T(8,128)S(1)}, f32[512,256]{1,0:T(8,128)}, u32[]{:S(2)}) copy-start(f32[512,256]{1,0:T(8,128)} %get-tuple-element.26.part_ref) | copy-start | bytes 1572868
  87.6 0.9 %copy-start.2 = (bf16[8,64,256]{2,1,0:T(8,128)(2,1)S(1)}, bf16[8,64,256]{2,1,0:T(8,128)(2,1)}, u32[]{:S(2)}) copy-start(bf16[8,64,256]{2,1,0:T(8,128)(2,1)} %get-tuple-element.25.arrived_ref) | copy-start | bytes 786436

commit v2 on v1

v2 whole, which is shorter than its diff:
```python
import functools
import jax
import jax.numpy as jnp
from jax import lax
from jax.experimental import pallas as pl
from jax.experimental.pallas import tpu as pltpu
from jax.sharding import PartitionSpec as P

F32, BF16 = jnp.float32, jnp.bfloat16
R = 64
SUB = 2
D = 256


def dot(a, b):
    return jnp.dot(a, b, preferred_element_type=F32)


def dot_rows(a, b):
    return lax.dot_general(a, b, (((0,), (0,)), ((), ())), preferred_element_type=F32)


def silu_parts(pre):
    gate = 0.5 * jnp.tanh(0.5 * pre) + 0.5
    hidden = pre * gate
    return hidden, gate + hidden * (1.0 - gate)


def centred(matrix):
    return matrix - jnp.mean(matrix, 1, keepdims=True)


def flipped(matrix):
    return jnp.transpose(matrix.astype(F32)).astype(BF16)


band_steps = (-1, -1, -1, 0, 0, 1, 1, 1)
sector_steps = (-1, 0, 1, -1, 1, -1, 0, 1)
MESH = pl.DeviceIdType.MESH


def neighbours(bands, sectors):
    band, sector = lax.axis_index("band"), lax.axis_index("sector")
    ahead = [
        (lax.rem(band + b + bands, bands), lax.rem(sector + s + sectors, sectors))
        for b, s in zip(band_steps, sector_steps)
    ]
    return ahead


def partners(bands, sectors):
    band, sector = lax.axis_index("band"), lax.axis_index("sector")
    core = lax.rem(band, 2)
    x = lax.rem(band // 2, 4)
    z = band // 8
    places = [((z * 4 + lax.rem(x + i, 4)) * 2 + core, sector) for i in (1, 2, 3)]
    places += [((lax.rem(z + i, 4) * 4 + x) * 2 + core, sector) for i in (1, 2, 3)]
    return places + [(band, lax.rem(sector + 2, 4))]


def picked(wanted, count):
    line = lax.broadcasted_iota(jnp.int32, (count, wanted.shape[1]), 0)
    return jnp.where(line == wanted, 1.0, 0.0).astype(BF16)


def sum_over(
    bands, sectors, share, back_ref, grads_ref, arrived_ref, out_ref,
    half_ref, one_ref, two_ref, three_ref, first_in, second_in, third_in,
    send_sem, recv_sem, core_sem, back_send, back_recv,
):
    ahead = neighbours(bands, sectors)
    band, sector = lax.axis_index("band"), lax.axis_index("sector")
    core = lax.rem(band, 2)
    x = lax.rem(band // 2, 4)
    z = band // 8
    at = {"x": x, "y": sector, "z": z}

    def place(axis, index):
        if axis == "x":
            return ((z * 4 + index) * 2 + core, sector)
        if axis == "z":
            return ((index * 4 + x) * 2 + core, sector)
        return (band, index)

    def others(axis):
        return [lax.rem(at[axis] + i, 4) for i in (1, 2, 3)]

    sibling = (band + 1 - 2 * core, sector)
    returns = []
    core_copy = pltpu.make_async_remote_copy(
        src_ref=grads_ref.at[1 - core], dst_ref=half_ref,
        send_sem=core_sem.at[0], recv_sem=core_sem.at[1],
        device_id=sibling, device_id_type=MESH,
    )
    core_copy.start()
    for j in range(8):
        returns.append(
            pltpu.make_async_remote_copy(
                src_ref=back_ref.at[j], dst_ref=arrived_ref.at[j],
                send_sem=back_send.at[j], recv_sem=back_recv.at[j],
                device_id=ahead[j], device_id_type=MESH,
            )
        )
        returns[-1].start()

    orders = (("x", "y", "z"), ("y", "z", "x"), ("z", "x", "y"))
    starts = [16 * sum(share[:p]) for p in range(3)]

    def exchange(stage, p, axis, source, target):
        copies = []
        for i, other in enumerate(others(axis)):
            copies.append(
                pltpu.make_async_remote_copy(
                    src_ref=source(other, i), dst_ref=target(i),
                    send_sem=send_sem.at[stage, p, i], recv_sem=recv_sem.at[stage, p, i],
                    device_id=place(axis, other), device_id_type=MESH,
                )
            )
            copies[-1].start()
        return copies

    def finish(copies):
        for copy in copies:
            copy.wait()

    core_copy.wait()
    one_ref[...] = (grads_ref[core].astype(F32) + half_ref[...].astype(F32)).astype(BF16)

    live = []
    for p in range(3):
        m, axis = share[p], orders[p][0]
        live.append(exchange(
            0, p, axis,
            lambda other, i, p=p, m=m: one_ref.at[pl.ds(starts[p] + other * (4 * m), 4 * m)],
            lambda i, p=p, m=m: first_in.at[i, pl.ds(4 * sum(share[:p]), 4 * m)],
        ))
    for p in range(3):
        m, axis, low = share[p], orders[p][0], 4 * sum(share[:p])
        finish(live[p])
        total = one_ref[pl.ds(starts[p] + at[axis] * (4 * m), 4 * m)].astype(F32)
        for i in range(3):
            total += first_in[i, low : low + 4 * m].astype(F32)
        two_ref[low : low + 4 * m] = total.astype(BF16)
        live[p] = exchange(
            1, p, orders[p][1],
            lambda other, i, low=low, m=m: two_ref.at[pl.ds(low + other * m, m)],
            lambda i, p=p, m=m: second_in.at[i, pl.ds(sum(share[:p]), m)],
        )
    for p in range(3):
        m, axis, low, mid = share[p], orders[p][1], sum(share[:p]), 4 * sum(share[:p])
        finish(live[p])
        total = two_ref[pl.ds(mid + at[axis] * m, m)].astype(F32)
        for i in range(3):
            total += second_in[i, low : low + m].astype(F32)
        three_ref[low : low + m] = total.astype(BF16)
        third = orders[p][2]
        third_in[at[third], low : low + m] = total.astype(BF16)
        live[p] = exchange(
            2, p, third,
            lambda other, i, low=low, m=m: three_ref.at[pl.ds(low, m)],
            lambda i, low=low, m=m, third=third: third_in.at[at[third], pl.ds(low, m)],
        )
    for p in range(3):
        m, low = share[p], sum(share[:p])
        finish(live[p])
        total = third_in[0, low : low + m].astype(F32)
        for i in range(1, 4):
            total += third_in[i, low : low + m].astype(F32)
        spot = starts[p] + at[orders[p][0]] * (4 * m) + at[orders[p][1]] * m
        out_ref[core, pl.ds(spot, m)] = total.astype(BF16)
        live[p] = exchange(
            3, p, orders[p][1],
            lambda other, i, spot=spot, m=m: out_ref.at[core, pl.ds(spot, m)],
            lambda i, spot=spot, m=m: out_ref.at[core, pl.ds(spot, m)],
        )
    for p in range(3):
        m = share[p]
        finish(live[p])
        spot = starts[p] + at[orders[p][0]] * (4 * m)
        live[p] = exchange(
            4, p, orders[p][0],
            lambda other, i, spot=spot, m=m: out_ref.at[core, pl.ds(spot, 4 * m)],
            lambda i, spot=spot, m=m: out_ref.at[core, pl.ds(spot, 4 * m)],
        )
    last = []
    for p in range(3):
        finish(live[p])
        spot, m = starts[p], 16 * share[p]
        last.append(pltpu.make_async_remote_copy(
            src_ref=out_ref.at[core, pl.ds(spot, m)], dst_ref=out_ref.at[core, pl.ds(spot, m)],
            send_sem=core_sem.at[2 + p], recv_sem=core_sem.at[5 + p],
            device_id=sibling, device_id_type=MESH,
        ))
        last[-1].start()
    finish(returns)
    finish(last)


def layer_kernel(
    bands, sectors, steps, slots, scale, share,
    own_ref, rows_ref, edge_ref, slot_ref, mask_ref,
    w_ein, b_e, w_eout, g_e, w_nin, b_n, w_nout, g_n, ncot_ref, ecot_ref,
    nnew_ref, enew_ref, egrad_ref, ngrad_ref, gein_ref, geout_ref, gnin_ref, gnout_ref,
    x_ref, xt_ref, g_ref, dz_ref, dpre_ref, wcat_ref, weo_ref, weot_ref, wet_ref, recv_ref, parts_ref, partst_ref,
    column_ref, line_ref, hid_ref, dsil_ref, xh_ref, rm_ref, gath_ref, dgath_ref,
    acc_ref, gout_ref, gd_ref, down_ref, gnode_ref,
    far_ref, out_ref, back_ref, arrived_ref, grads_ref, sums_ref,
    half_ref, one_ref, two_ref, three_ref, first_in, second_in, third_in,
    fetch_send, fetch_recv, send_sem, recv_sem, core_sem, back_send, back_recv,
):
    t = pl.program_id(0)
    rows = R * slots
    n = own_ref.shape[0]
    table = n + far_ref.shape[0] * far_ref.shape[1]
    seg = D + table

    tile_rows = slots * R

    def spread_rows(ref, base):
        upper = lax.broadcasted_iota(jnp.int32, (8, ref.shape[1]), 0) < 4
        pieces = []
        for pair in range(R // 2):
            a = jnp.broadcast_to(ref[pl.ds(base + 2 * pair, 1), :], (8, ref.shape[1]))
            b = jnp.broadcast_to(ref[pl.ds(base + 2 * pair + 1, 1), :], (8, ref.shape[1]))
            pieces += [a, jnp.where(upper, a, b), b]
        return jnp.concatenate(pieces, axis=0)

    @pl.when(t == 0)
    def _():
        ahead = neighbours(bands, sectors)
        barrier = pltpu.get_barrier_semaphore()
        everyone = ahead + partners(bands, sectors)
        for place in everyone:
            pl.semaphore_signal(barrier, inc=1, device_id=place, device_id_type=MESH)
        node = own_ref[...]
        for j in range(8):
            choice = picked(rows_ref[0, j : j + 1, :], n)
            out_ref[j] = dot_rows(choice, node).astype(BF16)
        pl.semaphore_wait(barrier, len(everyone))
        copies = []
        for j in range(8):
            copies.append(
                pltpu.make_async_remote_copy(
                    src_ref=out_ref.at[j], dst_ref=far_ref.at[j],
                    send_sem=fetch_send.at[j], recv_sem=fetch_recv.at[j],
                    device_id=ahead[7 - j], device_id_type=MESH,
                )
            )
            copies[-1].start()
        e = lax.broadcasted_iota(jnp.int32, (R, rows), 1)
        r = lax.broadcasted_iota(jnp.int32, (R, rows), 0)
        gap = e - slots * r
        inside = (gap >= 0) & (gap < slots)
        g_ref[...] = jnp.where(inside, 1.0, 0.0).astype(BF16)
        ef = lax.broadcasted_iota(jnp.int32, (32, rows), 1).astype(F32)
        lf = lax.broadcasted_iota(jnp.int32, (32, rows), 0).astype(F32)
        k = ef - slots * jnp.floor((ef + 0.5) * (1.0 / slots))
        selt = jnp.where(lf == k, 32.0, 0.0) + jnp.where(lf == k + 16.0, 1.0, 0.0)
        ef = lax.broadcasted_iota(jnp.int32, (rows, 128), 0).astype(F32)
        lf = lax.broadcasted_iota(jnp.int32, (rows, 128), 1).astype(F32)
        k = ef - slots * jnp.floor((ef + 0.5) * (1.0 / slots))
        sel = jnp.where(lf == k, 1.0, 0.0)
        v = slot_ref[...] + 1024 * mask_ref[...]
        partst_ref[...] = jnp.zeros_like(partst_ref)
        partst_ref[0:slots, :] = (v >> 5).astype(F32)
        partst_ref[16 : 16 + slots, :] = (v & 31).astype(F32)
        parts = jnp.transpose(partst_ref[...])
        parts_ref[...] = parts.astype(BF16)
        partst_ref[0:slots, :] = v.astype(F32)
        down_ref[:, 0:128] = jnp.transpose(partst_ref[...])
        for tile in range(n // R):
            piece = dot_rows(parts_ref[tile * R : tile * R + R, 0:32], g_ref[...])
            line_ref[tile] = jnp.sum(piece * selt, 0, keepdims=True)
            spread = spread_rows(down_ref.at[:, 0:128], tile * R)
            column_ref[tile * rows : tile * rows + rows, :] = jnp.sum(spread * sel, 1, keepdims=True)
        wcat_ref[0:D, :] = w_ein[0:D, :]
        wcat_ref[D : D + n, :] = dot(own_ref[...], w_ein[D : 2 * D, :]).astype(BF16)
        recv_ref[...] = dot(own_ref[...], w_ein[2 * D :, :]) + b_e[...]
        weo = centred(w_eout[...].astype(F32))
        weo_ref[...] = weo.astype(BF16)
        weot_ref[...] = jnp.transpose(weo).astype(BF16)
        wet_ref[...] = flipped(w_ein[0:D, :])
        acc_ref[...] = jnp.zeros_like(acc_ref)
        gout_ref[...] = jnp.zeros_like(gout_ref)
        for copy in copies:
            copy.wait()
        far = far_ref[...].reshape(table - n, D)
        wcat_ref[D + n : seg, :] = dot(far, w_ein[D : 2 * D, :]).astype(BF16)

    def spots(step, s):
        at = step * (R * SUB) + s * R
        here = pl.ds(pl.multiple_of(at * slots, rows), rows)
        mine = pl.ds(pl.multiple_of(at, R), R)
        return here, mine, slice(s * rows, (s + 1) * rows)

    def first_half(s):
        here, mine, part = spots(t, s)
        x = x_ref.at[s]
        x[:, 0:D] = edge_ref[part, :]
        v = column_ref[here, :]
        real = v >= 1024.0
        slot = jnp.where(real, v - 1024.0, v)
        lane = lax.broadcasted_iota(jnp.int32, (rows, D), 1).astype(F32).astype(BF16)
        for block in range(table // D):
            wanted = (slot - float(block * D)).astype(BF16)
            x[:, D + block * D : 2 * D + block * D] = jnp.where(
                lane == wanted, jnp.ones((), BF16), jnp.zeros((), BF16)
            )
        base = pl.multiple_of(t * (R * SUB) + s * R, R)
        pre = dot(x[...], wcat_ref[...]) + spread_rows(recv_ref, base)
        return pre, jnp.where(real, 1.0, 0.0)

    def second_half(s, pre, keep):
        here, mine, part = spots(t, s)
        hidden, slope = silu_parts(pre)
        hidden = hidden.astype(BF16)
        hid_ref[here, :] = hidden
        dsil_ref[here, :] = slope.astype(BF16)
        c = dot(hidden, weo_ref[...])
        rstd = lax.rsqrt(jnp.mean(c * c, 1, keepdims=True) + 1e-05)
        normed = c * rstd
        xh_ref[here, :] = normed.astype(BF16)
        rm_ref[here, :] = rstd * keep
        update = normed * g_e[...] * keep
        enew_ref[part, :] = (edge_ref[part, :].astype(F32) + update).astype(BF16)
        gath_ref[mine, :] = dot(g_ref[...], update.astype(BF16)).astype(BF16)

    @pl.when(t < steps)
    def _():
        held = first_half(0)
        for s in range(1, SUB):
            following = first_half(s)
            second_half(s - 1, *held)
            held = following
        second_half(SUB - 1, *held)

    @pl.when(t == steps)
    def _():
        own = own_ref[...]
        gath = gath_ref[...]
        pre = dot(own, w_nin[0:D, :]) + dot(gath, w_nin[D:, :]) + b_n[...]
        hidden, slope = silu_parts(pre)
        hidden = hidden.astype(BF16)
        wno = centred(w_nout[...].astype(F32))
        c = dot(hidden, wno.astype(BF16))
        rstd = lax.rsqrt(jnp.mean(c * c, 1, keepdims=True) + 1e-05)
        normed = c * rstd
        nnew_ref[...] = (own.astype(F32) + normed * g_n[...]).astype(BF16)
        cot = ncot_ref[...].astype(F32)
        dx = cot * g_n[...]
        share = jnp.mean(dx * normed, 1, keepdims=True)
        dz = (rstd * (dx - normed * share)).astype(BF16)
        gnode_ref[2 * D : 3 * D, :] = centred(dot_rows(hidden, dz))
        dpre = (dot(dz, jnp.transpose(wno).astype(BF16)) * slope).astype(BF16)
        gnode_ref[0:D, :] = dot_rows(own, dpre)
        gnode_ref[D : 2 * D, :] = dot_rows(gath, dpre)
        down_ref[...] = cot + dot(dpre, flipped(w_nin[0:D, :]))
        dgath_ref[...] = dot(dpre, flipped(w_nin[D:, :]))

    def third_half(s):
        here, mine, part = spots(t - steps - 1, s)
        v = line_ref[(t - steps - 1) * SUB + s]
        slot = jnp.where(v >= 1024.0, v - 1024.0, v)
        xt_ref[0:D, part] = jnp.transpose(edge_ref[part, :])
        line = lax.broadcasted_iota(jnp.int32, (D, rows), 0).astype(F32).astype(BF16)
        for block in range(table // D):
            wanted = (slot - float(block * D)).astype(BF16)
            xt_ref[D + block * D : 2 * D + block * D, part] = jnp.where(
                line == wanted, jnp.ones((), BF16), jnp.zeros((), BF16)
            )
        cot = ecot_ref[part, :].astype(F32)
        base = pl.multiple_of((t - steps - 1) * (R * SUB) + s * R, R)
        dx = (cot + spread_rows(dgath_ref, base)) * g_e[...]
        normed = xh_ref[here, :].astype(F32)
        share_of = jnp.mean(dx * normed, 1, keepdims=True)
        dz = (rm_ref[here, :] * (dx - normed * share_of)).astype(BF16)
        dz_ref[part, :] = dz
        dpre = (dot(dz, weot_ref[...]) * dsil_ref[here, :].astype(F32)).astype(BF16)
        dpre_ref[part, :] = dpre
        egrad_ref[part, :] = (cot + dot(dpre, wet_ref[...])).astype(BF16)
        gd_ref[mine, :] = dot(g_ref[...], dpre).astype(BF16)

    @pl.when(t > steps)
    def _():
        for s in range(SUB):
            third_half(s)
        span = pl.ds(pl.multiple_of((t - steps - 1) * (rows * SUB), rows), rows * SUB)
        gout_ref[...] += dot_rows(hid_ref[span, :], dz_ref[...])
        acc_ref[...] += dot(xt_ref[...], dpre_ref[...])

    @pl.when(t == 2 * steps)
    def _():
        own = own_ref[...]
        near = acc_ref[D : D + n, :].astype(BF16)
        far = acc_ref[D + n : seg, :].astype(BF16)
        wst = flipped(w_ein[D : 2 * D, :])
        back_ref[...] = dot(far, wst).astype(BF16).reshape(back_ref.shape)
        gd = gd_ref[...]
        down_ref[...] += dot(near, wst) + dot(gd, flipped(w_ein[2 * D :, :]))
        g_s = dot_rows(own, near) + dot_rows(far_ref[...].reshape(table - n, D), far)
        g_r = dot_rows(own, gd)
        whole = [acc_ref[0:D, :], g_s, g_r, centred(gout_ref[...])]
        whole += [gnode_ref[i * D : (i + 1) * D, :] for i in range(3)]
        at = 0
        for piece in whole:
            for i in range(D // 16):
                for j in range(2):
                    grads_ref[at // 112, at % 112] = piece[16 * i : 16 * i + 16, 128 * j : 128 * j + 128].astype(BF16)
                    at += 1
        sum_over(
            bands, sectors, share, back_ref, grads_ref, arrived_ref, sums_ref,
            half_ref, one_ref, two_ref, three_ref, first_in, second_in, third_in,
            send_sem, recv_sem, core_sem, back_send, back_recv,
        )
        total = down_ref[...]
        for j in range(8):
            total += dot(picked(rows_ref[0, j : j + 1, :], n), arrived_ref[j])
        ngrad_ref[...] = total
        at = 0
        for out in (gein_ref, geout_ref, gnin_ref, gnout_ref):
            for i in range(out.shape[0] // 16):
                for j in range(2):
                    out[16 * i : 16 * i + 16, 128 * j : 128 * j + 128] = sums_ref[at // 112, at % 112].astype(F32) * scale
                    at += 1


def layer_call(bands, sectors, node, rows_in, edge, slot, mask, w_ein, b_e, w_eout, g_e, w_nin, b_n, w_nout, g_n, ncot, ecot):
    n, d = node.shape
    slots = slot.shape[1]
    rows = R * slots
    tiles = n // (R * SUB)
    cap = rows_in.shape[2]
    table = n + 8 * cap
    unit = 7
    share = (3, 2, 2)
    scale = float(bands * sectors * n * slots) ** (-0.5)
    half = 16 * unit
    tile = (16, 128)
    seg = d + table
    total = n * slots
    whole = pl.BlockSpec(memory_space=pltpu.VMEM)
    stream_e = pl.BlockSpec((rows * SUB, d), lambda t: (jnp.where(t < tiles, t, jnp.maximum(t - tiles - 1, 0)), 0))
    first = pl.BlockSpec((rows * SUB, d), lambda t: (jnp.minimum(t, tiles - 1), 0))
    second = pl.BlockSpec((rows * SUB, d), lambda t: (jnp.maximum(t - tiles - 1, 0), 0))
    tiles_all = 7 * (d // 16) * (d // 128)
    flops = 2 * total * d * (d * 8 + 2 * table)
    return pl.pallas_call(
        functools.partial(layer_kernel, bands, sectors, tiles, slots, scale, share),
        grid=(2 * tiles + 1,),
        in_specs=[whole, whole, stream_e] + [whole] * 11 + [second],
        out_specs=[whole, first, second] + [whole] * 5,
        out_shape=[
            jax.ShapeDtypeStruct((n, d), BF16),
            jax.ShapeDtypeStruct((total, d), BF16),
            jax.ShapeDtypeStruct((total, d), BF16),
            jax.ShapeDtypeStruct((n, d), F32),
            jax.ShapeDtypeStruct((3 * d, d), F32),
            jax.ShapeDtypeStruct((d, d), F32),
            jax.ShapeDtypeStruct((2 * d, d), F32),
            jax.ShapeDtypeStruct((d, d), F32),
        ],
        scratch_shapes=[
            pltpu.VMEM((SUB, rows, seg), BF16),
            pltpu.VMEM((seg, SUB * rows), BF16),
            pltpu.VMEM((R, rows), BF16),
            pltpu.VMEM((SUB * rows, d), BF16),
            pltpu.VMEM((SUB * rows, d), BF16),
            pltpu.VMEM((seg, d), BF16),
            pltpu.VMEM((d, d), BF16),
            pltpu.VMEM((d, d), BF16),
            pltpu.VMEM((d, d), BF16),
            pltpu.VMEM((n, d), F32),
            pltpu.VMEM((n, 128), BF16),
            pltpu.VMEM((128, n), F32),
            pltpu.VMEM((total, 1), F32),
            pltpu.VMEM((n // R, 1, rows), F32),
            pltpu.VMEM((total, d), BF16),
            pltpu.VMEM((total, d), BF16),
            pltpu.VMEM((total, d), BF16),
            pltpu.VMEM((total, 1), F32),
            pltpu.VMEM((n, d), BF16),
            pltpu.VMEM((n, d), F32),
            pltpu.VMEM((seg, d), F32),
            pltpu.VMEM((d, d), F32),
            pltpu.VMEM((n, d), BF16),
            pltpu.VMEM((n, d), F32),
            pltpu.VMEM((3 * d, d), F32),
            pltpu.VMEM((8, cap, d), BF16),
            pltpu.VMEM((8, cap, d), BF16),
            pltpu.VMEM((8, cap, d), BF16),
            pltpu.VMEM((8, cap, d), BF16),
            pltpu.VMEM((2, half) + tile, BF16),
            pltpu.VMEM((2, half) + tile, BF16),
            pltpu.VMEM((half,) + tile, BF16),
            pltpu.VMEM((half,) + tile, BF16),
            pltpu.VMEM((half // 4,) + tile, BF16),
            pltpu.VMEM((unit,) + tile, BF16),
            pltpu.VMEM((3, half // 4) + tile, BF16),
            pltpu.VMEM((3, unit) + tile, BF16),
            pltpu.VMEM((4, unit) + tile, BF16),
            pltpu.SemaphoreType.DMA((8,)),
            pltpu.SemaphoreType.DMA((8,)),
            pltpu.SemaphoreType.DMA((5, 3, 3)),
            pltpu.SemaphoreType.DMA((5, 3, 3)),
            pltpu.SemaphoreType.DMA((8,)),
            pltpu.SemaphoreType.DMA((8,)),
            pltpu.SemaphoreType.DMA((8,)),
        ],
        compiler_params=pltpu.CompilerParams(
            vmem_limit_bytes=60 * 1024 * 1024, collective_id=0, has_side_effects=True
        ),
        cost_estimate=pl.CostEstimate(flops=flops, bytes_accessed=5 * total * d * 2, transcendentals=total * d),
    )(node, rows_in, edge, slot.T, mask.T, w_ein, b_e.reshape(1, -1), w_eout, g_e.reshape(1, -1), w_nin, b_n.reshape(1, -1), w_nout, g_n.reshape(1, -1), ncot, ecot)


def solution(mesh):
    bands, sectors = mesh.shape["band"], mesh.shape["sector"]

    def local(node, edge, slot, mask, rows, w_ein, b_e, w_eout, g_e, w_nin, b_n, w_nout, g_n, ncot, ecot):
        nnew, enew, egrad, ngrad, gein, geout, gnin, gnout = layer_call(
            bands, sectors, node, rows, edge, slot, mask,
            w_ein, b_e, w_eout, g_e, w_nin, b_n, w_nout, g_n, ncot, ecot,
        )
        return nnew, enew, ngrad, egrad, gein, geout, gnin, gnout

    split = P(("band", "sector"), None)
    in_specs = (split,) * 4 + (P(("band", "sector"), None, None),) + (P(),) * 8 + (split, split)
    out_specs = (split,) * 4 + (P(),) * 4
    return jax.shard_map(local, mesh=mesh, in_specs=in_specs, out_specs=out_specs, check_vma=False)
```

time: 91.1 us -> 79.9 us (0.88)
  Pallas kernels: 83.6 us -> 67.9 us
  local copies, waits for them, and re-layouts: 6.38 us -> 11.1 us
    pallas_call x4 -> x1, Pallas kernels: 83.6 us -> 67.9 us  [layer_call(): pl.pallas_call(functools.partial(layer_kernel, bands, sectors, tiles, slo...]
    unnamed x10 -> x20, local copies, waits for them, and re-layouts: 6.38 us -> 11.1 us
where the time goes in v2:
time: 79.9 us; the launch traced here: 79.7 us
  Pallas kernels  67.9 us (85%)
  local copies, waits for them, and re-layouts  11.1 us (14%)
    pallas_call x1, Pallas kernels, layer_call(): pl.pallas_call(functools.partial(layer_kernel, bands, sectors, tiles, slo...  67.9 us
    unnamed x20, local copies, waits for them, and re-layouts  11.1 us

profile of v2, /device:TPU:1, one launch (start us, length us, event | category | flops | bytes accessed | tf_op | source)
XLA Modules:
  0.0 79.7 jit_solution(13669289451619135301)
XLA Ops:
  0.6 67.9 %shard_map.206 = (bf16[512,256]{1,0:T(8,128)(2,1)}, bf16[6144,256]{1,0:T(8,128)(2,1)}, bf16[6144,256]{1,0:T(8,128)(2,1)}, f32[512,256]{1,0:T(8,128)}, f32[768,25...) custom-call(bf16[512,256]{1,0:T(8,128)(2,1)} %own_ref.1, s32[1,8,64]{2,1,0:T(8,128)} %rows_ref.1, ...), custom_call_target="tpu_custom_call" | custom-call | flops 12884901888 | bytes 15728640 | tf_op jit(solution)/shard_map/pallas_call | solution.py:447
  68.5 1.7 %copy.31 = bf16[512,256]{1,0:T(8,128)(2,1)} copy(bf16[512,256]{1,0:T(8,128)(2,1)} %get-tuple-element.32) | data formatting | bytes 524288
  70.2 0.0 copy-start.3
  70.2 0.0 copy-start
  70.2 3.9 %copy.32 = bf16[6144,256]{1,0:T(8,128)(2,1)} copy(bf16[6144,256]{1,0:T(8,128)(2,1)} %get-tuple-element.33) | data formatting | bytes 6291456
  74.1 0.0 copy-done.3
  74.1 0.8 copy.33
  74.9 0.0 copy-done
  74.9 0.0 copy-start.1
  74.9 0.0 copy-start.5
  74.9 0.0 copy-start.2
  74.9 1.7 %copy.34 = bf16[6144,256]{1,0:T(8,128)(2,1)} copy(bf16[6144,256]{1,0:T(8,128)(2,1)S(1)} %copy-done) | data formatting | bytes 6291456
  76.6 0.0 copy-done.1
  76.6 0.0 copy-start.4
  76.6 0.9 %copy.35 = f32[768,256]{1,0:T(8,128)} copy(f32[768,256]{1,0:T(8,128)S(1)} %copy-done.1) | data formatting | bytes 1572864
  77.5 0.0 copy-done.5
  77.5 0.7 copy.36
  78.2 0.0 copy-done.2
  78.2 0.8 copy.37
  79.0 0.0 copy-done.4
  79.0 0.7 copy.38
Async XLA Ops:
  70.2 3.9 %copy-start.3 = (f32[512,256]{1,0:T(8,128)S(1)}, f32[512,256]{1,0:T(8,128)}, u32[]{:S(2)}) copy-start(f32[512,256]{1,0:T(8,128)} %get-tuple-element.34) | copy-start | bytes 1572868
  70.2 4.7 %copy-start = (bf16[6144,256]{1,0:T(8,128)(2,1)S(1)}, bf16[6144,256]{1,0:T(8,128)(2,1)}, u32[]{:S(2)}) copy-start(bf16[6144,256]{1,0:T(8,128)(2,1)} %get-tuple-element.35) | copy-start | bytes 9437188
  74.9 1.7 %copy-start.1 = (f32[768,256]{1,0:T(8,128)S(1)}, f32[768,256]{1,0:T(8,128)}, u32[]{:S(2)}) copy-start(f32[768,256]{1,0:T(8,128)} %get-tuple-element.36) | copy-start | bytes 2359300
  74.9 2.6 %copy-start.5 = (f32[256,256]{1,0:T(8,128)S(1)}, f32[256,256]{1,0:T(8,128)}, u32[]{:S(2)}) copy-start(f32[256,256]{1,0:T(8,128)} %get-tuple-element.37) | copy-start | bytes 786436
  74.9 3.3 %copy-start.2 = (f32[512,256]{1,0:T(8,128)S(1)}, f32[512,256]{1,0:T(8,128)}, u32[]{:S(2)}) copy-start(f32[512,256]{1,0:T(8,128)} %get-tuple-element.38) | copy-start | bytes 1572868
  76.6 2.4 %copy-start.4 = (f32[256,256]{1,0:T(8,128)S(1)}, f32[256,256]{1,0:T(8,128)}, u32[]{:S(2)}) copy-start(f32[256,256]{1,0:T(8,128)} %get-tuple-element.39) | copy-start | bytes 786436

commit v3 on v1

--- a/solution.py
+++ b/solution.py
@@ -8,6 +8,7 @@
 
 F32, BF16 = jnp.float32, jnp.bfloat16
 R = 64
+SUB = 4
 D = 256
 
 
@@ -34,12 +35,12 @@
 
 
 def layer_kernel(
-    tiles, slots,
+    steps, slots,
     own_ref, far_ref, edge_ref, slot_ref, mask_ref,
     w_ein, b_e, w_eout, g_e, w_nin, b_n, w_nout, g_n, ncot_ref, ecot_ref,
     nnew_ref, enew_ref, egrad_ref, ngrad_ref, back_ref, grads_ref,
-    x_ref, xt_ref, wcat_ref, weo_ref, weot_ref, wet_ref, recv_ref, parts_ref,
-    sel_ref, selt_ref, hid_ref, dsil_ref, xh_ref, rm_ref, gath_ref, dgath_ref,
+    x_ref, xt_ref, g_ref, dz_ref, dpre_ref, wcat_ref, weo_ref, weot_ref, wet_ref, recv_ref, value_ref, parts_ref, partst_ref,
+    sel_ref, line_ref, hid_ref, dsil_ref, xh_ref, rm_ref, gath_ref, dgath_ref,
     acc_ref, gout_ref, gd_ref, down_ref, gnode_ref,
 ):
     t = pl.program_id(0)
@@ -48,33 +49,42 @@
     table = n + far_ref.shape[0]
     seg = D + table
 
+    def spread_rows(ref, base):
+        upper = lax.broadcasted_iota(jnp.int32, (8, ref.shape[1]), 0) < 4
+        pieces = []
+        for pair in range(R // 2):
+            a = jnp.broadcast_to(ref[pl.ds(base + 2 * pair, 1), :], (8, ref.shape[1]))
+            b = jnp.broadcast_to(ref[pl.ds(base + 2 * pair + 1, 1), :], (8, ref.shape[1]))
+            pieces += [a, jnp.where(upper, a, b), b]
+        return jnp.concatenate(pieces, axis=0)
+
     @pl.when(t == 0)
     def _():
-        e = lax.broadcasted_iota(jnp.int32, (rows, 128), 0)
-        l = lax.broadcasted_iota(jnp.int32, (rows, 128), 1)
-        r = jnp.where(l >= R, l - R, l)
-        gap = e - slots * r
-        inside = (gap >= 0) & (gap < slots)
-        x_ref[:, seg : seg + 128] = jnp.where(inside, 1.0, 0.0).astype(BF16)
-        ef = e.astype(F32)
-        k = ef - slots * jnp.floor((ef + 0.5) * (1.0 / slots))
-        lf = l.astype(F32)
-        sel_ref[...] = jnp.where(lf == k, 32.0, 0.0) + jnp.where(lf == k + 12.0, 1.0, 0.0)
         e = lax.broadcasted_iota(jnp.int32, (R, rows), 1)
         r = lax.broadcasted_iota(jnp.int32, (R, rows), 0)
         gap = e - slots * r
         inside = (gap >= 0) & (gap < slots)
-        xt_ref[seg : seg + R, :] = jnp.where(inside, 1.0, 0.0).astype(BF16)
+        g_ref[...] = jnp.where(inside, 1.0, 0.0).astype(BF16)
         ef = lax.broadcasted_iota(jnp.int32, (32, rows), 1).astype(F32)
         lf = lax.broadcasted_iota(jnp.int32, (32, rows), 0).astype(F32)
         k = ef - slots * jnp.floor((ef + 0.5) * (1.0 / slots))
-        selt_ref[...] = jnp.where(lf == k, 32.0, 0.0) + jnp.where(lf == k + 12.0, 1.0, 0.0)
+        selt = jnp.where(lf == k, 32.0, 0.0) + jnp.where(lf == k + 16.0, 1.0, 0.0)
+        ef = lax.broadcasted_iota(jnp.int32, (rows, 128), 0).astype(F32)
+        lf = lax.broadcasted_iota(jnp.int32, (rows, 128), 1).astype(F32)
+        k = ef - slots * jnp.floor((ef + 0.5) * (1.0 / slots))
+        sel_ref[...] = jnp.where(lf == k, 1.0, 0.0)
         v = slot_ref[...] + 1024 * mask_ref[...]
+        partst_ref[...] = jnp.zeros_like(partst_ref)
+        partst_ref[0:slots, :] = v.astype(F32)
+        value_ref[...] = jnp.transpose(partst_ref[...])
         high = (v >> 5).astype(F32)
         low = (v & 31).astype(F32)
-        parts_ref[...] = jnp.concatenate(
-            [high, low, jnp.zeros((n, 128 - 2 * slots), F32)], axis=1
-        ).astype(BF16)
+        parts_ref[...] = jnp.zeros_like(parts_ref)
+        parts_ref[0:16, :] = jnp.concatenate([high, jnp.zeros((16 - slots, n), F32)], axis=0).astype(BF16)
+        parts_ref[16:32, :] = jnp.concatenate([low, jnp.zeros((16 - slots, n), F32)], axis=0).astype(BF16)
+        for tile in range(n // R):
+            piece = dot(parts_ref[0:32, tile * R : tile * R + R], g_ref[...])
+            line_ref[tile] = jnp.sum(piece * selt, 0, keepdims=True)
         wcat_ref[0:D, :] = w_ein[0:D, :]
         wcat_ref[D : D + n, :] = dot(own_ref[...], w_ein[D : 2 * D, :]).astype(BF16)
         wcat_ref[D + n : seg, :] = dot(far_ref[...], w_ein[D : 2 * D, :]).astype(BF16)
@@ -86,27 +96,31 @@
         acc_ref[...] = jnp.zeros_like(acc_ref)
         gout_ref[...] = jnp.zeros_like(gout_ref)
 
-    @pl.when(t < tiles)
-    def _():
-        here = pl.ds(pl.multiple_of(t * rows, rows), rows)
-        mine = pl.ds(pl.multiple_of(t * R, R), R)
-        edges = edge_ref[...]
-        x_ref[:, 0:D] = edges
-        spread = dot(x_ref[:, seg : seg + R], parts_ref[mine, :])
-        v = jnp.sum(spread * sel_ref[...], 1, keepdims=True)
+    def spots(step, s):
+        at = step * (R * SUB) + s * R
+        here = pl.ds(pl.multiple_of(at * slots, rows), rows)
+        mine = pl.ds(pl.multiple_of(at, R), R)
+        return here, mine, slice(s * rows, (s + 1) * rows)
+
+    def first_half(s):
+        here, mine, part = spots(t, s)
+        x = x_ref.at[s]
+        x[:, 0:D] = edge_ref[part, :]
+        base = pl.multiple_of(t * (R * SUB) + s * R, R)
+        v = jnp.sum(spread_rows(value_ref, base) * sel_ref[...], 1, keepdims=True)
         real = v >= 1024.0
         slot = jnp.where(real, v - 1024.0, v)
         lane = lax.broadcasted_iota(jnp.int32, (rows, D), 1).astype(F32).astype(BF16)
         for block in range(table // D):
             wanted = (slot - float(block * D)).astype(BF16)
-            x_ref[:, D + block * D : 2 * D + block * D] = jnp.where(
+            x[:, D + block * D : 2 * D + block * D] = jnp.where(
                 lane == wanted, jnp.ones((), BF16), jnp.zeros((), BF16)
             )
-        recv = recv_ref[mine, :]
-        high = recv.astype(BF16)
-        wcat_ref[seg : seg + R, :] = high
-        wcat_ref[seg + R : seg + 2 * R, :] = (recv - high.astype(F32)).astype(BF16)
-        pre = dot(x_ref[...], wcat_ref[...])
+        pre = dot(x[...], wcat_ref[...]) + spread_rows(recv_ref, base)
+        return pre, jnp.where(real, 1.0, 0.0)
+
+    def second_half(s, pre, keep):
+        here, mine, part = spots(t, s)
         hidden, slope = silu_parts(pre)
         hidden = hidden.astype(BF16)
         hid_ref[here, :] = hidden
@@ -114,14 +128,22 @@
         c = dot(hidden, weo_ref[...])
         rstd = lax.rsqrt(jnp.mean(c * c, 1, keepdims=True) + 1e-05)
         normed = c * rstd
-        keep = jnp.where(real, 1.0, 0.0)
         xh_ref[here, :] = normed.astype(BF16)
         rm_ref[here, :] = rstd * keep
         update = normed * g_e[...] * keep
-        enew_ref[...] = (edges.astype(F32) + update).astype(BF16)
-        gath_ref[mine, :] = dot(xt_ref[seg : seg + R, :], update.astype(BF16)).astype(BF16)
-
-    @pl.when(t == tiles)
+        enew_ref[part, :] = (edge_ref[part, :].astype(F32) + update).astype(BF16)
+        gath_ref[mine, :] = dot(g_ref[...], update.astype(BF16)).astype(BF16)
+
+    @pl.when(t < steps)
+    def _():
+        held = first_half(0)
+        for s in range(1, SUB):
+            following = first_half(s)
+            second_half(s - 1, *held)
+            held = following
+        second_half(SUB - 1, *held)
+
+    @pl.when(t == steps)
     def _():
         own = own_ref[...]
         gath = gath_ref[...]
@@ -142,36 +164,40 @@
         gnode_ref[0:D, :] = dot_rows(own, dpre)
         gnode_ref[D : 2 * D, :] = dot_rows(gath, dpre)
         down_ref[...] = cot + dot(dpre, flipped(w_nin[0:D, :]))
-        dgath_ref[...] = dot(dpre, flipped(w_nin[D:, :])).astype(BF16)
-
-    @pl.when(t > tiles)
-    def _():
-        u = t - tiles - 1
-        here = pl.ds(pl.multiple_of(u * rows, rows), rows)
-        mine = pl.ds(pl.multiple_of(u * R, R), R)
-        cot = ecot_ref[...].astype(F32)
-        spread = dot(x_ref[:, seg : seg + R], dgath_ref[mine, :])
-        dx = (cot + spread) * g_e[...]
-        normed = xh_ref[here, :].astype(F32)
-        share = jnp.mean(dx * normed, 1, keepdims=True)
-        dz = (rm_ref[here, :] * (dx - normed * share)).astype(BF16)
-        gout_ref[...] += dot_rows(hid_ref[here, :], dz)
-        dpre = (dot(dz, weot_ref[...]) * dsil_ref[here, :].astype(F32)).astype(BF16)
-        egrad_ref[...] = (cot + dot(dpre, wet_ref[...])).astype(BF16)
-        part = dot_rows(parts_ref[mine, 0:32], xt_ref[seg : seg + R, :])
-        v = jnp.sum(part * selt_ref[...], 0, keepdims=True)
+        dgath_ref[...] = dot(dpre, flipped(w_nin[D:, :]))
+
+    def third_half(s):
+        here, mine, part = spots(t - steps - 1, s)
+        v = line_ref[(t - steps - 1) * SUB + s]
         slot = jnp.where(v >= 1024.0, v - 1024.0, v)
-        xt_ref[0:D, :] = jnp.transpose(edge_ref[...])
+        xt_ref[0:D, part] = jnp.transpose(edge_ref[part, :])
         line = lax.broadcasted_iota(jnp.int32, (D, rows), 0).astype(F32).astype(BF16)
         for block in range(table // D):
             wanted = (slot - float(block * D)).astype(BF16)
-            xt_ref[D + block * D : 2 * D + block * D, :] = jnp.where(
+            xt_ref[D + block * D : 2 * D + block * D, part] = jnp.where(
                 line == wanted, jnp.ones((), BF16), jnp.zeros((), BF16)
             )
-        acc_ref[...] += dot(xt_ref[0:seg, :], dpre)
-        gd_ref[mine, :] = dot(xt_ref[seg : seg + R, :], dpre).astype(BF16)
-
-    @pl.when(t == 2 * tiles)
+        cot = ecot_ref[part, :].astype(F32)
+        base = pl.multiple_of((t - steps - 1) * (R * SUB) + s * R, R)
+        dx = (cot + spread_rows(dgath_ref, base)) * g_e[...]
+        normed = xh_ref[here, :].astype(F32)
+        share_of = jnp.mean(dx * normed, 1, keepdims=True)
+        dz = (rm_ref[here, :] * (dx - normed * share_of)).astype(BF16)
+        dz_ref[part, :] = dz
+        dpre = (dot(dz, weot_ref[...]) * dsil_ref[here, :].astype(F32)).astype(BF16)
+        dpre_ref[part, :] = dpre
+        egrad_ref[part, :] = (cot + dot(dpre, wet_ref[...])).astype(BF16)
+        gd_ref[mine, :] = dot(g_ref[...], dpre).astype(BF16)
+
+    @pl.when(t > steps)
+    def _():
+        for s in range(SUB):
+            third_half(s)
+        span = pl.ds(pl.multiple_of((t - steps - 1) * (rows * SUB), rows), rows * SUB)
+        gout_ref[...] += dot_rows(hid_ref[span, :], dz_ref[...])
+        acc_ref[...] += dot(xt_ref[...], dpre_ref[...])
+
+    @pl.when(t == 2 * steps)
     def _():
         own = own_ref[...]
         near = acc_ref[D : D + n, :].astype(BF16)
@@ -196,14 +222,14 @@
     n, d = node.shape
     slots = slot.shape[1]
     rows = R * slots
-    tiles = n // R
+    tiles = n // (R * SUB)
     table = n + far.shape[0]
     seg = d + table
     total = n * slots
     whole = pl.BlockSpec(memory_space=pltpu.VMEM)
-    stream_e = pl.BlockSpec((rows, d), lambda t: (jnp.where(t < tiles, t, jnp.maximum(t - tiles - 1, 0)), 0))
-    first = pl.BlockSpec((rows, d), lambda t: (jnp.minimum(t, tiles - 1), 0))
-    second = pl.BlockSpec((rows, d), lambda t: (jnp.maximum(t - tiles - 1, 0), 0))
+    stream_e = pl.BlockSpec((rows * SUB, d), lambda t: (jnp.where(t < tiles, t, jnp.maximum(t - tiles - 1, 0)), 0))
+    first = pl.BlockSpec((rows * SUB, d), lambda t: (jnp.minimum(t, tiles - 1), 0))
+    second = pl.BlockSpec((rows * SUB, d), lambda t: (jnp.maximum(t - tiles - 1, 0), 0))
     tiles_all = 7 * (d // 16) * (d // 128)
     flops = 2 * total * d * (d * 8 + 2 * table)
     return pl.pallas_call(
@@ -220,31 +246,37 @@
             jax.ShapeDtypeStruct((tiles_all, 16, 128), BF16),
         ],
         scratch_shapes=[
-            pltpu.VMEM((rows, seg + 2 * R), BF16),
-            pltpu.VMEM((seg + R, rows), BF16),
-            pltpu.VMEM((seg + 2 * R, d), BF16),
+            pltpu.VMEM((SUB, rows, seg), BF16),
+            pltpu.VMEM((seg, SUB * rows), BF16),
+            pltpu.VMEM((R, rows), BF16),
+            pltpu.VMEM((SUB * rows, d), BF16),
+            pltpu.VMEM((SUB * rows, d), BF16),
+            pltpu.VMEM((seg, d), BF16),
             pltpu.VMEM((d, d), BF16),
             pltpu.VMEM((d, d), BF16),
             pltpu.VMEM((d, d), BF16),
             pltpu.VMEM((n, d), F32),
-            pltpu.VMEM((n, 128), BF16),
+            pltpu.VMEM((n, 128), F32),
+            pltpu.VMEM((32, n), BF16),
+            pltpu.VMEM((128, n), F32),
             pltpu.VMEM((rows, 128), F32),
-            pltpu.VMEM((32, rows), F32),
+            pltpu.VMEM((n // R, 1, rows), F32),
             pltpu.VMEM((total, d), BF16),
             pltpu.VMEM((total, d), BF16),
             pltpu.VMEM((total, d), BF16),
             pltpu.VMEM((total, 1), F32),
             pltpu.VMEM((n, d), BF16),
-            pltpu.VMEM((n, d), BF16),
+            pltpu.VMEM((n, d), F32),
             pltpu.VMEM((seg, d), F32),
             pltpu.VMEM((d, d), F32),
             pltpu.VMEM((n, d), BF16),
             pltpu.VMEM((n, d), F32),
             pltpu.VMEM((3 * d, d), F32),
         ],
-        compiler_params=pltpu.CompilerParams(vmem_limit_bytes=56 * 1024 * 1024),
+        compiler_params=pltpu.CompilerParams(vmem_limit_bytes=60 * 1024 * 1024),
         cost_estimate=pl.CostEstimate(flops=flops, bytes_accessed=5 * total * d * 2, transcendentals=total * d),
-    )(node, far, edge, slot, mask, w_ein, b_e.reshape(1, -1), w_eout, g_e.reshape(1, -1), w_nin, b_n.reshape(1, -1), w_nout, g_n.reshape(1, -1), ncot, ecot)
+    )(node, far, edge, slot.T, mask.T, w_ein, b_e.reshape(1, -1), w_eout, g_e.reshape(1, -1), w_nin, b_n.reshape(1, -1), w_nout, g_n.reshape(1, -1), ncot, ecot)
+
 
 band_steps = (-1, -1, -1, 0, 0, 1, 1, 1)
 sector_steps = (-1, 0, 1, -1, 1, -1, 0, 1)
@@ -258,13 +290,6 @@
         for b, s in zip(band_steps, sector_steps)
     ]
     return ahead
-
-
-def greet(places):
-    barrier = pltpu.get_barrier_semaphore()
-    for place in places:
-        pl.semaphore_signal(barrier, inc=1, device_id=place, device_id_type=MESH)
-    pl.semaphore_wait(barrier, len(places))
 
 
 def picked(wanted, count):
@@ -312,14 +337,16 @@
             pltpu.SemaphoreType.DMA((8,)),
             pltpu.SemaphoreType.DMA((8,)),
         ],
-        compiler_params=pltpu.CompilerParams(collective_id=0, has_side_effects=True),
+        compiler_params=pltpu.CompilerParams(
+            collective_id=0, has_side_effects=True, vmem_limit_bytes=60 * 1024 * 1024
+        ),
     )(node, rows)
 
 
 def sum_kernel(
     bands, sectors, share, back_ref, grads_ref, arrived_ref, out_ref,
     half_ref, one_ref, two_ref, three_ref, first_in, second_in, third_in,
-    send_sem, recv_sem, core_sem, back_send, back_recv,
+    mine_ref, send_sem, recv_sem, core_sem, back_send, back_recv, load_sem,
 ):
     ahead = neighbours(bands, sectors)
     band, sector = lax.axis_index("band"), lax.axis_index("sector")
@@ -341,7 +368,12 @@
     sibling = (band + 1 - 2 * core, sector)
     peers = [place("x", i) for i in others("x")] + [place("z", i) for i in others("z")]
     peers += [place("y", lax.rem(sector + 2, 4))]
-    greet(ahead + peers)
+    barrier = pltpu.get_barrier_semaphore()
+    for spot in ahead + peers:
+        pl.semaphore_signal(barrier, inc=1, device_id=spot, device_id_type=MESH)
+    load = pltpu.make_async_copy(grads_ref.at[core], mine_ref, load_sem)
+    load.start()
+    pl.semaphore_wait(barrier, len(ahead + peers))
 
     returns = []
     core_copy = pltpu.make_async_remote_copy(
@@ -380,8 +412,9 @@
         for copy in copies:
             copy.wait()
 
+    load.wait()
     core_copy.wait()
-    one_ref[...] = (grads_ref[core].astype(F32) + half_ref[...].astype(F32)).astype(BF16)
+    one_ref[...] = (mine_ref[...].astype(F32) + half_ref[...].astype(F32)).astype(BF16)
 
     live = []
     for p in range(3):
@@ -458,11 +491,12 @@
     unit = half // 16
     share = (unit - 2 * (unit // 3), unit // 3, unit // 3)
     whole = pl.BlockSpec(memory_space=pltpu.VMEM)
+    there = pl.BlockSpec(memory_space=pl.ANY)
     tile = grads.shape[1:]
     return pl.pallas_call(
         functools.partial(sum_kernel, bands, sectors, share),
-        in_specs=[whole, whole],
-        out_specs=[whole, whole],
+        in_specs=[there, there],
+        out_specs=[there, whole],
         out_shape=[
             jax.ShapeDtypeStruct(back.shape, BF16),
             jax.ShapeDtypeStruct((2, half) + tile, BF16),
@@ -475,22 +509,38 @@
             pltpu.VMEM((3, half // 4) + tile, BF16),
             pltpu.VMEM((3, unit) + tile, BF16),
             pltpu.VMEM((4, unit) + tile, BF16),
+            pltpu.VMEM((half,) + tile, BF16),
             pltpu.SemaphoreType.DMA((5, 3, 3)),
             pltpu.SemaphoreType.DMA((5, 3, 3)),
             pltpu.SemaphoreType.DMA((8,)),
             pltpu.SemaphoreType.DMA((8,)),
             pltpu.SemaphoreType.DMA((8,)),
+            pltpu.SemaphoreType.DMA,
         ],
-        compiler_params=pltpu.CompilerParams(collective_id=1, has_side_effects=True),
+        compiler_params=pltpu.CompilerParams(
+            collective_id=1, has_side_effects=True, vmem_limit_bytes=60 * 1024 * 1024
+        ),
     )(back, grads.reshape((2, half) + tile))
 
 
-def close_kernel(scale, rows_ref, arrived_ref, part_ref, sums_ref, ngrad_ref, *outs):
+def close_kernel(scale, rows_ref, arrived_hbm, part_hbm, sums_hbm, ngrad_ref, *refs):
+    outs, (arrived_ref, part_ref, sums_ref, sem) = refs[:4], refs[4:]
+    loads = [
+        pltpu.make_async_copy(part_hbm, part_ref, sem.at[0]),
+        pltpu.make_async_copy(arrived_hbm, arrived_ref, sem.at[1]),
+        pltpu.make_async_copy(sums_hbm, sums_ref, sem.at[2]),
+    ]
+    for load in loads:
+        load.start()
     n = part_ref.shape[0]
+    chosen = [picked(rows_ref[0, j : j + 1, :], n) for j in range(8)]
+    loads[0].wait()
+    loads[1].wait()
     total = part_ref[...]
     for j in range(8):
-        total += dot(picked(rows_ref[0, j : j + 1, :], n), arrived_ref[j])
+        total += dot(chosen[j], arrived_ref[j])
     ngrad_ref[...] = total
+    loads[2].wait()
     at = 0
     for out in outs:
         for i in range(out.shape[0] // 16):
@@ -502,14 +552,22 @@
 def close_call(scale, rows, arrived, part, sums):
     d = part.shape[1]
     whole = pl.BlockSpec(memory_space=pltpu.VMEM)
+    there = pl.BlockSpec(memory_space=pl.ANY)
     outs = [part.shape, (3 * d, d), (d, d), (2 * d, d), (d, d)]
+    sums = sums.reshape((-1,) + sums.shape[2:])
     return pl.pallas_call(
         functools.partial(close_kernel, scale),
-        in_specs=[whole] * 4,
+        in_specs=[whole, there, there, there],
         out_specs=[whole] * 5,
         out_shape=[jax.ShapeDtypeStruct(shape, F32) for shape in outs],
-        compiler_params=pltpu.CompilerParams(vmem_limit_bytes=32 * 1024 * 1024),
-    )(rows, arrived, part, sums.reshape((-1,) + sums.shape[2:]))
+        scratch_shapes=[
+            pltpu.VMEM(arrived.shape, BF16),
+            pltpu.VMEM(part.shape, F32),
+            pltpu.VMEM(sums.shape, BF16),
+            pltpu.SemaphoreType.DMA((3,)),
+        ],
+        compiler_params=pltpu.CompilerParams(vmem_limit_bytes=60 * 1024 * 1024),
+    )(rows, arrived, part, sums)
 
 
 def solution(mesh):

time: 91.1 us -> 76.8 us (0.84)
  Pallas kernels: 83.6 us -> 76 us
  local copies, waits for them, and re-layouts: 6.38 us -> 0 us
    pallas_call x1, Pallas kernels: 35.2 us -> 26.5 us  [layer_call(): pl.pallas_call(functools.partial(layer_kernel, tiles, slots), grid=(2 * t...]
    unnamed x10 -> x0, local copies, waits for them, and re-layouts: 6.38 us -> none
    pallas_call x1, Pallas kernels: 2.08 us -> 3.99 us  [close_call(): pl.pallas_call(functools.partial(close_kernel, scale), in_specs=[whole, t...]
    pallas_call x1, Pallas kernels: 32.6 us -> 31.7 us  [sum_call(): pl.pallas_call(functools.partial(sum_kernel, bands, sectors, share), in_s...]
where the time goes in v3:
time: 76.8 us; the launch traced here: 76.6 us
  Pallas kernels  76 us (99%)
    pallas_call x1, Pallas kernels, sum_call(): pl.pallas_call(functools.partial(sum_kernel, bands, sectors, share), in_s...  31.7 us
    pallas_call x1, Pallas kernels, layer_call(): pl.pallas_call(functools.partial(layer_kernel, tiles, slots), grid=(2 * t...  26.5 us
    pallas_call x1, Pallas kernels, fetch_call(): pl.pallas_call(functools.partial(fetch_kernel, bands, sectors), in_specs=...  13.7 us
    pallas_call x1, Pallas kernels, close_call(): pl.pallas_call(functools.partial(close_kernel, scale), in_specs=[whole, t...  3.99 us

profile of v3, /device:TPU:1, one launch (start us, length us, event | category | flops | bytes accessed | tf_op | source)
XLA Modules:
  0.0 76.6 jit_solution(17774867504354229012)
XLA Ops:
  0.6 13.7 %shard_map.206 = bf16[8,64,256]{2,1,0:T(8,128)(2,1)} custom-call(bf16[512,256]{1,0:T(8,128)(2,1)} %own_ref.1, s32[1,8,64]{2,1,0:T(8,128)} %rows_ref.3), custom_call_target="tpu_custom_call" | custom-call | tf_op jit(solution)/shard_map/pallas_call | solution.py:330
  14.4 26.5 %shard_map.207 = (bf16[512,256]{1,0:T(8,128)(2,1)}, bf16[6144,256]{1,0:T(8,128)(2,1)}, bf16[6144,256]{1,0:T(8,128)(2,1)}, f32[512,256]{1,0:T(8,128)}, bf16[8,64,...) custom-call(bf16[512,256]{1,0:T(8,128)(2,1)} %own_ref.1, bf16[512,256]{1,0:T(8,128)(2,1)} %bitcast.11, ...), custom_call_target="tpu_custom_call" | custom-call | flops 12884901888 | bytes 15728640 | tf_op jit(solution)/shard_map/pallas_call | solution.py:235
  40.9 31.7 %shard_map.208 = (bf16[8,64,256]{2,1,0:T(8,128)(2,1)}, bf16[2,112,16,128]{3,2,1,0:T(8,128)(2,1)}) custom-call(bf16[8,64,256]{2,1,0:T(8,128)(2,1)} %get-tuple-element.23.back_ref, bf16[2,112,16,128]{3,2,1,0:T(8,128)(2,1)} %bitcast.9), custom_call_target="tpu_custom_call" | custom-call | tf_op jit(solution)/shard_map/pallas_call | solution.py:496
  72.6 4.0 %shard_map.209 = (f32[512,256]{1,0:T(8,128)}, f32[768,256]{1,0:T(8,128)}, f32[256,256]{1,0:T(8,128)}, f32[512,256]{1,0:T(8,128)}, f32[256,256]{1,0:T(8,128)}) custom-call(s32[1,8,64]{2,1,0:T(8,128)} %rows_ref.3, bf16[8,64,256]{2,1,0:T(8,128)(2,1)} %get-tuple-element.25.arrived_hbm, f32[512,256]{1,0:T(8,128)} %get-tuple-element.26.part_hbm, ...), custom_call_target="tpu_custom_call" | custom-call | tf_op jit(solution)/shard_map/pallas_call | solution.py:558

commit v4 on v3

--- a/solution.py
+++ b/solution.py
@@ -37,11 +37,12 @@
 def layer_kernel(
     steps, slots,
     own_ref, far_ref, edge_ref, slot_ref, mask_ref,
-    w_ein, b_e, w_eout, g_e, w_nin, b_n, w_nout, g_n, ncot_ref, ecot_ref,
-    nnew_ref, enew_ref, egrad_ref, ngrad_ref, back_ref, grads_ref,
+    w_ein, b_e, w_eout, g_e, nin_hbm, b_n, nout_hbm, g_n, ncot_hbm, ecot_ref,
+    nnew_hbm, enew_ref, egrad_hbm, ngrad_hbm, back_hbm, grads_ref,
     x_ref, xt_ref, g_ref, dz_ref, dpre_ref, wcat_ref, weo_ref, weot_ref, wet_ref, recv_ref, value_ref, parts_ref, partst_ref,
     sel_ref, line_ref, hid_ref, dsil_ref, xh_ref, rm_ref, gath_ref, dgath_ref,
     acc_ref, gout_ref, gd_ref, down_ref, gnode_ref,
+    egrad_ref, w_nin, w_nout, ncot_ref, nnew_ref, back_ref, egrad_sem, node_sem,
 ):
     t = pl.program_id(0)
     rows = R * slots
@@ -58,8 +59,23 @@
             pieces += [a, jnp.where(upper, a, b), b]
         return jnp.concatenate(pieces, axis=0)
 
+    late = [
+        pltpu.make_async_copy(nin_hbm, w_nin, node_sem.at[0]),
+        pltpu.make_async_copy(nout_hbm, w_nout, node_sem.at[1]),
+        pltpu.make_async_copy(ncot_hbm, ncot_ref, node_sem.at[2]),
+    ]
+    nnew_copy = pltpu.make_async_copy(nnew_ref, nnew_hbm, node_sem.at[3])
+    down_copy = pltpu.make_async_copy(down_ref, ngrad_hbm, node_sem.at[4])
+    back_copy = pltpu.make_async_copy(back_ref, back_hbm, node_sem.at[5])
+
+    def egrad_copy(step, s):
+        span = pl.ds(pl.multiple_of((step * SUB + s) * rows, rows), rows)
+        return pltpu.make_async_copy(egrad_ref.at[s * rows : (s + 1) * rows, :], egrad_hbm.at[span, :], egrad_sem.at[s])
+
     @pl.when(t == 0)
     def _():
+        for copy in late:
+            copy.start()
         e = lax.broadcasted_iota(jnp.int32, (R, rows), 1)
         r = lax.broadcasted_iota(jnp.int32, (R, rows), 0)
         gap = e - slots * r
@@ -145,6 +161,8 @@
 
     @pl.when(t == steps)
     def _():
+        for copy in late:
+            copy.wait()
         own = own_ref[...]
         gath = gath_ref[...]
         pre = dot(own, w_nin[0:D, :]) + dot(gath, w_nin[D:, :]) + b_n[...]
@@ -155,6 +173,7 @@
         rstd = lax.rsqrt(jnp.mean(c * c, 1, keepdims=True) + 1e-05)
         normed = c * rstd
         nnew_ref[...] = (own.astype(F32) + normed * g_n[...]).astype(BF16)
+        nnew_copy.start()
         cot = ncot_ref[...].astype(F32)
         dx = cot * g_n[...]
         share = jnp.mean(dx * normed, 1, keepdims=True)
@@ -187,7 +206,13 @@
         dpre = (dot(dz, weot_ref[...]) * dsil_ref[here, :].astype(F32)).astype(BF16)
         dpre_ref[part, :] = dpre
         egrad_ref[part, :] = (cot + dot(dpre, wet_ref[...])).astype(BF16)
+        egrad_copy(t - steps - 1, s).start()
         gd_ref[mine, :] = dot(g_ref[...], dpre).astype(BF16)
+
+    @pl.when(t > steps + 1)
+    def _():
+        for s in range(SUB):
+            egrad_copy(t - steps - 2, s).wait()
 
     @pl.when(t > steps)
     def _():
@@ -204,8 +229,10 @@
         far = acc_ref[D + n : seg, :].astype(BF16)
         wst = flipped(w_ein[D : 2 * D, :])
         back_ref[...] = dot(far, wst).astype(BF16).reshape(back_ref.shape)
+        back_copy.start()
         gd = gd_ref[...]
-        ngrad_ref[...] = down_ref[...] + dot(near, wst) + dot(gd, flipped(w_ein[2 * D :, :]))
+        down_ref[...] += dot(near, wst) + dot(gd, flipped(w_ein[2 * D :, :]))
+        down_copy.start()
         g_s = dot_rows(own, near) + dot_rows(far_ref[...], far)
         g_r = dot_rows(own, gd)
         whole = [acc_ref[0:D, :], g_s, g_r, centred(gout_ref[...])]
@@ -216,6 +243,10 @@
                 for j in range(2):
                     grads_ref[at] = piece[16 * i : 16 * i + 16, 128 * j : 128 * j + 128].astype(BF16)
                     at += 1
+        for s in range(SUB):
+            egrad_copy(steps - 1, s).wait()
+        for copy in (nnew_copy, down_copy, back_copy):
+            copy.wait()
 
 
 def layer_call(node, far, edge, slot, mask, w_ein, b_e, w_eout, g_e, w_nin, b_n, w_nout, g_n, ncot, ecot):
@@ -227,6 +258,7 @@
     seg = d + table
     total = n * slots
     whole = pl.BlockSpec(memory_space=pltpu.VMEM)
+    there = pl.BlockSpec(memory_space=pl.ANY)
     stream_e = pl.BlockSpec((rows * SUB, d), lambda t: (jnp.where(t < tiles, t, jnp.maximum(t - tiles - 1, 0)), 0))
     first = pl.BlockSpec((rows * SUB, d), lambda t: (jnp.minimum(t, tiles - 1), 0))
     second = pl.BlockSpec((rows * SUB, d), lambda t: (jnp.maximum(t - tiles - 1, 0), 0))
@@ -235,8 +267,8 @@
     return pl.pallas_call(
         functools.partial(layer_kernel, tiles, slots),
         grid=(2 * tiles + 1,),
-        in_specs=[whole, whole, stream_e] + [whole] * 11 + [second],
-        out_specs=[whole, first, second, whole, whole, whole],
+        in_specs=[whole, whole, stream_e] + [whole] * 6 + [there, whole, there, whole, there, second],
+        out_specs=[there, first, there, there, there, whole],
         out_shape=[
             jax.ShapeDtypeStruct((n, d), BF16),
             jax.ShapeDtypeStruct((total, d), BF16),
@@ -272,6 +304,14 @@
             pltpu.VMEM((n, d), BF16),
             pltpu.VMEM((n, d), F32),
             pltpu.VMEM((3 * d, d), F32),
+            pltpu.VMEM((SUB * rows, d), BF16),
+            pltpu.VMEM((2 * d, d), BF16),
+            pltpu.VMEM((d, d), BF16),
+            pltpu.VMEM((n, d), BF16),
+            pltpu.VMEM((n, d), BF16),
+            pltpu.VMEM((8, far.shape[0] // 8, d), BF16),
+            pltpu.SemaphoreType.DMA((SUB,)),
+            pltpu.SemaphoreType.DMA((6,)),
         ],
         compiler_params=pltpu.CompilerParams(vmem_limit_bytes=60 * 1024 * 1024),
         cost_estimate=pl.CostEstimate(flops=flops, bytes_accessed=5 * total * d * 2, transcendentals=total * d),
@@ -297,11 +337,16 @@
     return jnp.where(line == wanted, 1.0, 0.0).astype(BF16)
 
 
-def fetch_kernel(bands, sectors, node_ref, rows_ref, far_ref, out_ref, send_sem, recv_sem):
+def fetch_kernel(
+    bands, sectors, node_hbm, rows_ref, far_ref, out_ref, node_ref, send_sem, recv_sem, load_sem
+):
     ahead = neighbours(bands, sectors)
     barrier = pltpu.get_barrier_semaphore()
     for place in ahead:
         pl.semaphore_signal(barrier, inc=1, device_id=place, device_id_type=MESH)
+    load = pltpu.make_async_copy(node_hbm, node_ref, load_sem)
+    load.start()
+    load.wait()
     node = node_ref[...]
     for j in range(8):
         choice = picked(rows_ref[0, j : j + 1, :], node.shape[0])
@@ -327,15 +372,18 @@
 def fetch_call(bands, sectors, node, rows):
     cap, d = rows.shape[2], node.shape[1]
     whole = pl.BlockSpec(memory_space=pltpu.VMEM)
+    there = pl.BlockSpec(memory_space=pl.ANY)
     return pl.pallas_call(
         functools.partial(fetch_kernel, bands, sectors),
-        in_specs=[whole, whole],
-        out_specs=whole,
+        in_specs=[there, whole],
+        out_specs=there,
         out_shape=jax.ShapeDtypeStruct((8, cap, d), BF16),
         scratch_shapes=[
             pltpu.VMEM((8, cap, d), BF16),
+            pltpu.VMEM(node.shape, BF16),
             pltpu.SemaphoreType.DMA((8,)),
             pltpu.SemaphoreType.DMA((8,)),
+            pltpu.SemaphoreType.DMA,
         ],
         compiler_params=pltpu.CompilerParams(
             collective_id=0, has_side_effects=True, vmem_limit_bytes=60 * 1024 * 1024
@@ -523,30 +571,43 @@
     )(back, grads.reshape((2, half) + tile))
 
 
-def close_kernel(scale, rows_ref, arrived_hbm, part_hbm, sums_hbm, ngrad_ref, *refs):
-    outs, (arrived_ref, part_ref, sums_ref, sem) = refs[:4], refs[4:]
+def close_kernel(scale, rows_ref, arrived_hbm, part_hbm, sums_hbm, *refs):
+    targets, (arrived_ref, part_ref, sums_ref, ngrad_ref), outs = refs[:5], refs[5:9], refs[9:13]
+    load_sem, store_sem = refs[13:]
+    spans, at = [], 0
+    for out in outs:
+        size = out.shape[0] // 8
+        spans.append((at, size))
+        at += size
     loads = [
-        pltpu.make_async_copy(part_hbm, part_ref, sem.at[0]),
-        pltpu.make_async_copy(arrived_hbm, arrived_ref, sem.at[1]),
-        pltpu.make_async_copy(sums_hbm, sums_ref, sem.at[2]),
+        pltpu.make_async_copy(sums_hbm.at[start : start + size], sums_ref.at[start : start + size], load_sem.at[i])
+        for i, (start, size) in enumerate(spans)
     ]
+    loads.append(pltpu.make_async_copy(part_hbm, part_ref, load_sem.at[4]))
+    loads.append(pltpu.make_async_copy(arrived_hbm, arrived_ref, load_sem.at[5]))
     for load in loads:
         load.start()
+    stores = [
+        pltpu.make_async_copy(ref, target, store_sem.at[i])
+        for i, (ref, target) in enumerate(zip(outs + (ngrad_ref,), targets[1:] + targets[:1]))
+    ]
     n = part_ref.shape[0]
     chosen = [picked(rows_ref[0, j : j + 1, :], n) for j in range(8)]
-    loads[0].wait()
-    loads[1].wait()
+    for i, (out, (start, size)) in enumerate(zip(outs, spans)):
+        loads[i].wait()
+        for tile in range(size):
+            r, l = 16 * (tile // 2), 128 * (tile % 2)
+            out[r : r + 16, l : l + 128] = sums_ref[start + tile].astype(F32) * scale
+        stores[i].start()
+    loads[4].wait()
+    loads[5].wait()
     total = part_ref[...]
     for j in range(8):
         total += dot(chosen[j], arrived_ref[j])
     ngrad_ref[...] = total
-    loads[2].wait()
-    at = 0
-    for out in outs:
-        for i in range(out.shape[0] // 16):
-            for j in range(out.shape[1] // 128):
-                out[16 * i : 16 * i + 16, 128 * j : 128 * j + 128] = sums_ref[at].astype(F32) * scale
-                at += 1
+    stores[4].start()
+    for store in stores:
+        store.wait()
 
 
 def close_call(scale, rows, arrived, part, sums):
@@ -558,14 +619,15 @@
     return pl.pallas_call(
         functools.partial(close_kernel, scale),
         in_specs=[whole, there, there, there],
-        out_specs=[whole] * 5,
+        out_specs=[there] * 5,
         out_shape=[jax.ShapeDtypeStruct(shape, F32) for shape in outs],
         scratch_shapes=[
             pltpu.VMEM(arrived.shape, BF16),
             pltpu.VMEM(part.shape, F32),
             pltpu.VMEM(sums.shape, BF16),
-            pltpu.SemaphoreType.DMA((3,)),
-        ],
+        ]
+        + [pltpu.VMEM(shape, F32) for shape in outs]
+        + [pltpu.SemaphoreType.DMA((6,)), pltpu.SemaphoreType.DMA((5,))],
         compiler_params=pltpu.CompilerParams(vmem_limit_bytes=60 * 1024 * 1024),
     )(rows, arrived, part, sums)
 

time: 76.8 us -> 75.3 us (0.980)
  Pallas kernels: 76 us -> 74.4 us
    pallas_call x1, Pallas kernels: 13.7 us -> 12.9 us  [fetch_call(): pl.pallas_call(functools.partial(fetch_kernel, bands, sectors), in_specs=...]
where the time goes in v4:
time: 75.3 us; the launch traced here: 75.1 us
  Pallas kernels  74.4 us (99%)
    pallas_call x1, Pallas kernels, sum_call(): pl.pallas_call(functools.partial(sum_kernel, bands, sectors, share), in_s...  31.7 us
    pallas_call x1, Pallas kernels, layer_call(): pl.pallas_call(functools.partial(layer_kernel, tiles, slots), grid=(2 * t...  26.2 us
    pallas_call x1, Pallas kernels, fetch_call(): pl.pallas_call(functools.partial(fetch_kernel, bands, sectors), in_specs=...  12.9 us
    pallas_call x1, Pallas kernels, close_call(): pl.pallas_call(functools.partial(close_kernel, scale), in_specs=[whole, t...  3.67 us

profile of v4, /device:TPU:1, one launch (start us, length us, event | category | flops | bytes accessed | tf_op | source)
XLA Modules:
  0.0 75.1 jit_solution(12218720562663714376)
XLA Ops:
  0.6 12.9 %shard_map.206 = bf16[8,64,256]{2,1,0:T(8,128)(2,1)} custom-call(bf16[512,256]{1,0:T(8,128)(2,1)} %own_ref.1, s32[1,8,64]{2,1,0:T(8,128)} %rows_ref.3), custom_call_target="tpu_custom_call" | custom-call | tf_op jit(solution)/shard_map/pallas_call | solution.py:376
  13.5 26.2 %shard_map.207 = (bf16[512,256]{1,0:T(8,128)(2,1)}, bf16[6144,256]{1,0:T(8,128)(2,1)}, bf16[6144,256]{1,0:T(8,128)(2,1)}, f32[512,256]{1,0:T(8,128)}, bf16[8,64,...) custom-call(bf16[512,256]{1,0:T(8,128)(2,1)} %own_ref.1, bf16[512,256]{1,0:T(8,128)(2,1)} %bitcast.11, ...), custom_call_target="tpu_custom_call" | custom-call | flops 12884901888 | bytes 15728640 | tf_op jit(solution)/shard_map/pallas_call | solution.py:267
  39.7 31.7 %shard_map.208 = (bf16[8,64,256]{2,1,0:T(8,128)(2,1)}, bf16[2,112,16,128]{3,2,1,0:T(8,128)(2,1)}) custom-call(bf16[8,64,256]{2,1,0:T(8,128)(2,1)} %get-tuple-element.23.back_ref, bf16[2,112,16,128]{3,2,1,0:T(8,128)(2,1)} %bitcast.9), custom_call_target="tpu_custom_call" | custom-call | tf_op jit(solution)/shard_map/pallas_call | solution.py:544
  71.4 3.7 %shard_map.209 = (f32[512,256]{1,0:T(8,128)}, f32[768,256]{1,0:T(8,128)}, f32[256,256]{1,0:T(8,128)}, f32[512,256]{1,0:T(8,128)}, f32[256,256]{1,0:T(8,128)}) custom-call(s32[1,8,64]{2,1,0:T(8,128)} %rows_ref.3, bf16[8,64,256]{2,1,0:T(8,128)(2,1)} %get-tuple-element.25.arrived_hbm, f32[512,256]{1,0:T(8,128)} %get-tuple-element.26.part_hbm, ...), custom_call_target="tpu_custom_call" | custom-call | tf_op jit(solution)/shard_map/pallas_call | solution.py:619

commit v5 on v4

--- a/solution.py
+++ b/solution.py
@@ -34,12 +34,29 @@
     return jnp.transpose(matrix.astype(F32)).astype(BF16)
 
 
+def spread_rows(ref, base):
+    upper = lax.broadcasted_iota(jnp.int32, (8, ref.shape[1]), 0) < 4
+    pieces = []
+    for pair in range(R // 2):
+        a = jnp.broadcast_to(ref[pl.ds(base + 2 * pair, 1), :], (8, ref.shape[1]))
+        b = jnp.broadcast_to(ref[pl.ds(base + 2 * pair + 1, 1), :], (8, ref.shape[1]))
+        pieces += [a, jnp.where(upper, a, b), b]
+    return jnp.concatenate(pieces, axis=0)
+
+
+def slot_lanes(rows, slots):
+    ef = lax.broadcasted_iota(jnp.int32, (rows, 128), 0).astype(F32)
+    lf = lax.broadcasted_iota(jnp.int32, (rows, 128), 1).astype(F32)
+    k = ef - slots * jnp.floor((ef + 0.5) * (1.0 / slots))
+    return jnp.where(lf == k, 1.0, 0.0)
+
+
 def layer_kernel(
     steps, slots,
-    own_ref, far_ref, edge_ref, slot_ref, mask_ref,
-    w_ein, b_e, w_eout, g_e, nin_hbm, b_n, nout_hbm, g_n, ncot_hbm, ecot_ref,
+    own_ref, far_ref, near_ref, edge_ref, slot_ref, mask_ref,
+    w_ein, w_eout, g_e, nin_hbm, b_n, nout_hbm, g_n, ncot_hbm, ecot_ref,
     nnew_hbm, enew_ref, egrad_hbm, ngrad_hbm, back_hbm, grads_ref,
-    x_ref, xt_ref, g_ref, dz_ref, dpre_ref, wcat_ref, weo_ref, weot_ref, wet_ref, recv_ref, value_ref, parts_ref, partst_ref,
+    x_ref, xt_ref, g_ref, dz_ref, dpre_ref, wcat_ref, weo_ref, weot_ref, wet_ref, value_ref, parts_ref, partst_ref,
     sel_ref, line_ref, hid_ref, dsil_ref, xh_ref, rm_ref, gath_ref, dgath_ref,
     acc_ref, gout_ref, gd_ref, down_ref, gnode_ref,
     egrad_ref, w_nin, w_nout, ncot_ref, nnew_ref, back_ref, egrad_sem, node_sem,
@@ -49,15 +66,6 @@
     n = own_ref.shape[0]
     table = n + far_ref.shape[0]
     seg = D + table
-
-    def spread_rows(ref, base):
-        upper = lax.broadcasted_iota(jnp.int32, (8, ref.shape[1]), 0) < 4
-        pieces = []
-        for pair in range(R // 2):
-            a = jnp.broadcast_to(ref[pl.ds(base + 2 * pair, 1), :], (8, ref.shape[1]))
-            b = jnp.broadcast_to(ref[pl.ds(base + 2 * pair + 1, 1), :], (8, ref.shape[1]))
-            pieces += [a, jnp.where(upper, a, b), b]
-        return jnp.concatenate(pieces, axis=0)
 
     late = [
         pltpu.make_async_copy(nin_hbm, w_nin, node_sem.at[0]),
@@ -85,10 +93,7 @@
         lf = lax.broadcasted_iota(jnp.int32, (32, rows), 0).astype(F32)
         k = ef - slots * jnp.floor((ef + 0.5) * (1.0 / slots))
         selt = jnp.where(lf == k, 32.0, 0.0) + jnp.where(lf == k + 16.0, 1.0, 0.0)
-        ef = lax.broadcasted_iota(jnp.int32, (rows, 128), 0).astype(F32)
-        lf = lax.broadcasted_iota(jnp.int32, (rows, 128), 1).astype(F32)
-        k = ef - slots * jnp.floor((ef + 0.5) * (1.0 / slots))
-        sel_ref[...] = jnp.where(lf == k, 1.0, 0.0)
+        sel_ref[...] = slot_lanes(rows, slots)
         v = slot_ref[...] + 1024 * mask_ref[...]
         partst_ref[...] = jnp.zeros_like(partst_ref)
         partst_ref[0:slots, :] = v.astype(F32)
@@ -101,10 +106,7 @@
         for tile in range(n // R):
             piece = dot(parts_ref[0:32, tile * R : tile * R + R], g_ref[...])
             line_ref[tile] = jnp.sum(piece * selt, 0, keepdims=True)
-        wcat_ref[0:D, :] = w_ein[0:D, :]
-        wcat_ref[D : D + n, :] = dot(own_ref[...], w_ein[D : 2 * D, :]).astype(BF16)
-        wcat_ref[D + n : seg, :] = dot(far_ref[...], w_ein[D : 2 * D, :]).astype(BF16)
-        recv_ref[...] = dot(own_ref[...], w_ein[2 * D :, :]) + b_e[...]
+        wcat_ref[...] = dot(far_ref[...], w_ein[D : 2 * D, :]).astype(BF16)
         weo = centred(w_eout[...].astype(F32))
         weo_ref[...] = weo.astype(BF16)
         weot_ref[...] = jnp.transpose(weo).astype(BF16)
@@ -121,18 +123,17 @@
     def first_half(s):
         here, mine, part = spots(t, s)
         x = x_ref.at[s]
-        x[:, 0:D] = edge_ref[part, :]
         base = pl.multiple_of(t * (R * SUB) + s * R, R)
         v = jnp.sum(spread_rows(value_ref, base) * sel_ref[...], 1, keepdims=True)
         real = v >= 1024.0
         slot = jnp.where(real, v - 1024.0, v)
         lane = lax.broadcasted_iota(jnp.int32, (rows, D), 1).astype(F32).astype(BF16)
-        for block in range(table // D):
-            wanted = (slot - float(block * D)).astype(BF16)
-            x[:, D + block * D : 2 * D + block * D] = jnp.where(
+        for block in range((table - n) // D):
+            wanted = (slot - float(n + block * D)).astype(BF16)
+            x[:, block * D : D + block * D] = jnp.where(
                 lane == wanted, jnp.ones((), BF16), jnp.zeros((), BF16)
             )
-        pre = dot(x[...], wcat_ref[...]) + spread_rows(recv_ref, base)
+        pre = dot(x[...], wcat_ref[...]) + near_ref[part, :].astype(F32)
         return pre, jnp.where(real, 1.0, 0.0)
 
     def second_half(s, pre, keep):
@@ -249,9 +250,9 @@
             copy.wait()
 
 
-def layer_call(node, far, edge, slot, mask, w_ein, b_e, w_eout, g_e, w_nin, b_n, w_nout, g_n, ncot, ecot):
+def layer_call(node, far, near, edge, slot, mask, w_ein, w_eout, g_e, w_nin, b_n, w_nout, g_n, ncot, ecot):
     n, d = node.shape
-    slots = slot.shape[1]
+    slots = slot.shape[0]
     rows = R * slots
     tiles = n // (R * SUB)
     table = n + far.shape[0]
@@ -267,7 +268,7 @@
     return pl.pallas_call(
         functools.partial(layer_kernel, tiles, slots),
         grid=(2 * tiles + 1,),
-        in_specs=[whole, whole, stream_e] + [whole] * 6 + [there, whole, there, whole, there, second],
+        in_specs=[whole, whole, first, stream_e] + [whole] * 5 + [there, whole, there, whole, there, second],
         out_specs=[there, first, there, there, there, whole],
         out_shape=[
             jax.ShapeDtypeStruct((n, d), BF16),
@@ -278,16 +279,15 @@
             jax.ShapeDtypeStruct((tiles_all, 16, 128), BF16),
         ],
         scratch_shapes=[
-            pltpu.VMEM((SUB, rows, seg), BF16),
+            pltpu.VMEM((SUB, rows, table - n), BF16),
             pltpu.VMEM((seg, SUB * rows), BF16),
             pltpu.VMEM((R, rows), BF16),
             pltpu.VMEM((SUB * rows, d), BF16),
             pltpu.VMEM((SUB * rows, d), BF16),
-            pltpu.VMEM((seg, d), BF16),
+            pltpu.VMEM((table - n, d), BF16),
             pltpu.VMEM((d, d), BF16),
             pltpu.VMEM((d, d), BF16),
             pltpu.VMEM((d, d), BF16),
-            pltpu.VMEM((n, d), F32),
             pltpu.VMEM((n, 128), F32),
             pltpu.VMEM((32, n), BF16),
             pltpu.VMEM((128, n), F32),
@@ -315,7 +315,7 @@
         ],
         compiler_params=pltpu.CompilerParams(vmem_limit_bytes=60 * 1024 * 1024),
         cost_estimate=pl.CostEstimate(flops=flops, bytes_accessed=5 * total * d * 2, transcendentals=total * d),
-    )(node, far, edge, slot.T, mask.T, w_ein, b_e.reshape(1, -1), w_eout, g_e.reshape(1, -1), w_nin, b_n.reshape(1, -1), w_nout, g_n.reshape(1, -1), ncot, ecot)
+    )(node, far, near, edge, slot, mask, w_ein, w_eout, g_e.reshape(1, -1), w_nin, b_n.reshape(1, -1), w_nout, g_n.reshape(1, -1), ncot, ecot)
 
 
 band_steps = (-1, -1, -1, 0, 0, 1, 1, 1)
@@ -338,49 +338,94 @@
 
 
 def fetch_kernel(
-    bands, sectors, node_hbm, rows_ref, far_ref, out_ref, node_ref, send_sem, recv_sem, load_sem
+    bands, sectors, slots, node_hbm, rows_ref, slot_ref, w_ein, b_e, edge_ref, far_ref, near_ref,
+    out_ref, node_ref, wcat_ref, recv_ref, value_ref, flip_ref, sel_ref, x_ref,
+    send_sem, recv_sem, load_sem,
 ):
+    t = pl.program_id(0)
     ahead = neighbours(bands, sectors)
-    barrier = pltpu.get_barrier_semaphore()
-    for place in ahead:
-        pl.semaphore_signal(barrier, inc=1, device_id=place, device_id_type=MESH)
-    load = pltpu.make_async_copy(node_hbm, node_ref, load_sem)
-    load.start()
-    load.wait()
-    node = node_ref[...]
-    for j in range(8):
-        choice = picked(rows_ref[0, j : j + 1, :], node.shape[0])
-        out_ref[j] = dot_rows(choice, node).astype(BF16)
-    pl.semaphore_wait(barrier, 8)
-    copies = []
-    for j in range(8):
-        copies.append(
-            pltpu.make_async_remote_copy(
-                src_ref=out_ref.at[j],
-                dst_ref=far_ref.at[j],
-                send_sem=send_sem.at[j],
-                recv_sem=recv_sem.at[j],
-                device_id=ahead[7 - j],
-                device_id_type=MESH,
+    rows = R * slots
+    n = node_ref.shape[0]
+    copies = [
+        pltpu.make_async_remote_copy(
+            src_ref=out_ref.at[j],
+            dst_ref=far_ref.at[j],
+            send_sem=send_sem.at[j],
+            recv_sem=recv_sem.at[j],
+            device_id=ahead[7 - j],
+            device_id_type=MESH,
+        )
+        for j in range(8)
+    ]
+
+    @pl.when(t == 0)
+    def _():
+        barrier = pltpu.get_barrier_semaphore()
+        for place in ahead:
+            pl.semaphore_signal(barrier, inc=1, device_id=place, device_id_type=MESH)
+        load = pltpu.make_async_copy(node_hbm, node_ref, load_sem)
+        load.start()
+        load.wait()
+        node = node_ref[...]
+        for j in range(8):
+            choice = picked(rows_ref[0, j : j + 1, :], n)
+            out_ref[j] = dot_rows(choice, node).astype(BF16)
+        pl.semaphore_wait(barrier, 8)
+        for copy in copies:
+            copy.start()
+        wcat_ref[0:D, :] = w_ein[0:D, :]
+        wcat_ref[D : D + n, :] = dot(node, w_ein[D : 2 * D, :]).astype(BF16)
+        recv_ref[...] = dot(node, w_ein[2 * D :, :]) + b_e[...]
+        flip_ref[...] = jnp.zeros_like(flip_ref)
+        flip_ref[0:slots, :] = slot_ref[...].astype(F32)
+        value_ref[...] = jnp.transpose(flip_ref[...])
+        sel_ref[...] = slot_lanes(rows, slots)
+
+    for s in range(SUB):
+        base = pl.multiple_of(t * (R * SUB) + s * R, R)
+        x = x_ref.at[s]
+        x[:, 0:D] = edge_ref[s * rows : (s + 1) * rows, :]
+        slot = jnp.sum(spread_rows(value_ref, base) * sel_ref[...], 1, keepdims=True)
+        lane = lax.broadcasted_iota(jnp.int32, (rows, D), 1).astype(F32).astype(BF16)
+        for block in range(n // D):
+            wanted = (slot - float(block * D)).astype(BF16)
+            x[:, D + block * D : 2 * D + block * D] = jnp.where(
+                lane == wanted, jnp.ones((), BF16), jnp.zeros((), BF16)
             )
-        )
-        copies[-1].start()
-    for copy in copies:
-        copy.wait()
-
-
-def fetch_call(bands, sectors, node, rows):
-    cap, d = rows.shape[2], node.shape[1]
+        near = dot(x[...], wcat_ref[...]) + spread_rows(recv_ref, base)
+        near_ref[s * rows : (s + 1) * rows, :] = near.astype(BF16)
+
+    @pl.when(t == pl.num_programs(0) - 1)
+    def _():
+        for copy in copies:
+            copy.wait()
+
+
+def fetch_call(bands, sectors, node, rows_in, slot, w_ein, b_e, edge):
+    cap, (n, d) = rows_in.shape[2], node.shape
+    slots = slot.shape[0]
+    rows = R * slots
     whole = pl.BlockSpec(memory_space=pltpu.VMEM)
     there = pl.BlockSpec(memory_space=pl.ANY)
+    stream = pl.BlockSpec((rows * SUB, d), lambda t: (t, 0))
     return pl.pallas_call(
-        functools.partial(fetch_kernel, bands, sectors),
-        in_specs=[there, whole],
-        out_specs=there,
-        out_shape=jax.ShapeDtypeStruct((8, cap, d), BF16),
+        functools.partial(fetch_kernel, bands, sectors, slots),
+        grid=(n // (R * SUB),),
+        in_specs=[there, whole, whole, whole, whole, stream],
+        out_specs=[there, stream],
+        out_shape=[
+            jax.ShapeDtypeStruct((8, cap, d), BF16),
+            jax.ShapeDtypeStruct(edge.shape, BF16),
+        ],
         scratch_shapes=[
             pltpu.VMEM((8, cap, d), BF16),
-            pltpu.VMEM(node.shape, BF16),
+            pltpu.VMEM((n, d), BF16),
+            pltpu.VMEM((d + n, d), BF16),
+            pltpu.VMEM((n, d), F32),
+            pltpu.VMEM((n, 128), F32),
+            pltpu.VMEM((128, n), F32),
+            pltpu.VMEM((rows, 128), F32),
+            pltpu.VMEM((SUB, rows, d + n), BF16),
             pltpu.SemaphoreType.DMA((8,)),
             pltpu.SemaphoreType.DMA((8,)),
             pltpu.SemaphoreType.DMA,
@@ -388,7 +433,7 @@
         compiler_params=pltpu.CompilerParams(
             collective_id=0, has_side_effects=True, vmem_limit_bytes=60 * 1024 * 1024
         ),
-    )(node, rows)
+    )(node, rows_in, slot, w_ein, b_e.reshape(1, -1), edge)
 
 
 def sum_kernel(
@@ -637,10 +682,11 @@
 
     def local(node, edge, slot, mask, rows, w_ein, b_e, w_eout, g_e, w_nin, b_n, w_nout, g_n, ncot, ecot):
         n, d = node.shape
-        far = fetch_call(bands, sectors, node, rows)
+        slot_t, mask_t = slot.T, mask.T
+        far, near = fetch_call(bands, sectors, node, rows, slot_t, w_ein, b_e, edge)
         nnew, enew, egrad, part, back, grads = layer_call(
-            node, far.reshape(-1, d), edge, slot, mask,
-            w_ein, b_e, w_eout, g_e, w_nin, b_n, w_nout, g_n, ncot, ecot,
+            node, far.reshape(-1, d), near, edge, slot_t, mask_t,
+            w_ein, w_eout, g_e, w_nin, b_n, w_nout, g_n, ncot, ecot,
         )
         arrived, sums = sum_call(bands, sectors, back, grads)
         scale = float(bands * sectors * n * slot.shape[1]) ** (-0.5)

time: 75.3 us -> 76.9 us (1.021)
  Pallas kernels: 74.4 us -> 75.9 us
    pallas_call x1, Pallas kernels: 12.9 us -> 14.9 us  [fetch_call(): pl.pallas_call(functools.partial(fetch_kernel, bands, sectors, slots), gr...]
where the time goes in v5:
time: 76.9 us; the launch traced here: 76.7 us
  Pallas kernels  75.9 us (99%)
  between operations  0.82 us (1%)
    pallas_call x1, Pallas kernels, sum_call(): pl.pallas_call(functools.partial(sum_kernel, bands, sectors, share), in_s...  31.7 us
    pallas_call x1, Pallas kernels, layer_call(): pl.pallas_call(functools.partial(layer_kernel, tiles, slots), grid=(2 * t...  25.6 us
    pallas_call x1, Pallas kernels, fetch_call(): pl.pallas_call(functools.partial(fetch_kernel, bands, sectors, slots), gr...  14.9 us
    pallas_call x1, Pallas kernels, close_call(): pl.pallas_call(functools.partial(close_kernel, scale), in_specs=[whole, t...  3.66 us

profile of v5, /device:TPU:1, one launch (start us, length us, event | category | flops | bytes accessed | tf_op | source)
XLA Modules:
  0.0 76.7 jit_solution(2468260879209053211)
XLA Ops:
  0.6 14.9 %shard_map.206 = (bf16[8,64,256]{2,1,0:T(8,128)(2,1)}, bf16[6144,256]{1,0:T(8,128)(2,1)}) custom-call(bf16[512,256]{1,0:T(8,128)(2,1)} %own_ref.1, s32[1,8,64]{2,1,0:T(8,128)} %rows_ref.3, s32[12,512]{1,0:T(8,128)} %bitcast.11, bf16[768,256]{1,0:T(8,128)(2,1)} %w_ein.3, f32[1,256]{1,0:T(1,128)} %bitcast.13, bf16[6144,256]{1,0:T(8,128)(2,1)} %edge_ref.3), custom_call_target="tpu_custom_call" | custom-call | tf_op jit(solution)/shard_map/pallas_call | solution.py:411
  15.6 25.6 %shard_map.207 = (bf16[512,256]{1,0:T(8,128)(2,1)}, bf16[6144,256]{1,0:T(8,128)(2,1)}, bf16[6144,256]{1,0:T(8,128)(2,1)}, f32[512,256]{1,0:T(8,128)}, bf16[8,64,...) custom-call(bf16[512,256]{1,0:T(8,128)(2,1)} %own_ref.1, bf16[512,256]{1,0:T(8,128)(2,1)} %bitcast.14, ...), custom_call_target="tpu_custom_call" | custom-call | flops 12884901888 | bytes 15728640 | tf_op jit(solution)/shard_map/pallas_call | solution.py:268
  41.1 31.7 %shard_map.208 = (bf16[8,64,256]{2,1,0:T(8,128)(2,1)}, bf16[2,112,16,128]{3,2,1,0:T(8,128)(2,1)}) custom-call(bf16[8,64,256]{2,1,0:T(8,128)(2,1)} %get-tuple-element.27.back_ref, bf16[2,112,16,128]{3,2,1,0:T(8,128)(2,1)} %bitcast.9), custom_call_target="tpu_custom_call" | custom-call | tf_op jit(solution)/shard_map/pallas_call | solution.py:589
  72.9 3.7 %shard_map.209 = (f32[512,256]{1,0:T(8,128)}, f32[768,256]{1,0:T(8,128)}, f32[256,256]{1,0:T(8,128)}, f32[512,256]{1,0:T(8,128)}, f32[256,256]{1,0:T(8,128)}) custom-call(s32[1,8,64]{2,1,0:T(8,128)} %rows_ref.3, bf16[8,64,256]{2,1,0:T(8,128)(2,1)} %get-tuple-element.29.arrived_hbm, f32[512,256]{1,0:T(8,128)} %get-tuple-element.30.part_hbm, ...), custom_call_target="tpu_custom_call" | custom-call | tf_op jit(solution)/shard_map/pallas_call | solution.py:664

commit v6 on v4

--- a/solution.py
+++ b/solution.py
@@ -143,10 +143,11 @@
         dsil_ref[here, :] = slope.astype(BF16)
         c = dot(hidden, weo_ref[...])
         rstd = lax.rsqrt(jnp.mean(c * c, 1, keepdims=True) + 1e-05)
-        normed = c * rstd
+        kept = rstd * keep
+        normed = c * kept
         xh_ref[here, :] = normed.astype(BF16)
-        rm_ref[here, :] = rstd * keep
-        update = normed * g_e[...] * keep
+        rm_ref[here, :] = kept
+        update = normed * g_e[...]
         enew_ref[part, :] = (edge_ref[part, :].astype(F32) + update).astype(BF16)
         gath_ref[mine, :] = dot(g_ref[...], update.astype(BF16)).astype(BF16)
 
@@ -203,6 +204,10 @@
         share_of = jnp.mean(dx * normed, 1, keepdims=True)
         dz = (rm_ref[here, :] * (dx - normed * share_of)).astype(BF16)
         dz_ref[part, :] = dz
+        return cot, dz
+
+    def final_half(s, cot, dz):
+        here, mine, part = spots(t - steps - 1, s)
         dpre = (dot(dz, weot_ref[...]) * dsil_ref[here, :].astype(F32)).astype(BF16)
         dpre_ref[part, :] = dpre
         egrad_ref[part, :] = (cot + dot(dpre, wet_ref[...])).astype(BF16)
@@ -216,8 +221,12 @@
 
     @pl.when(t > steps)
     def _():
-        for s in range(SUB):
-            third_half(s)
+        held = third_half(0)
+        for s in range(1, SUB):
+            following = third_half(s)
+            final_half(s - 1, *held)
+            held = following
+        final_half(SUB - 1, *held)
         span = pl.ds(pl.multiple_of((t - steps - 1) * (rows * SUB), rows), rows * SUB)
         gout_ref[...] += dot_rows(hid_ref[span, :], dz_ref[...])
         acc_ref[...] += dot(xt_ref[...], dpre_ref[...])

time: 75.3 us -> 75.1 us (level)
  no operation moved by 1% of the time
where the time goes in v6:
time: 75.1 us; the launch traced here: 74.8 us
  Pallas kernels  74.2 us (99%)
    pallas_call x1, Pallas kernels, sum_call(): pl.pallas_call(functools.partial(sum_kernel, bands, sectors, share), in_s...  31.7 us
    pallas_call x1, Pallas kernels, layer_call(): pl.pallas_call(functools.partial(layer_kernel, tiles, slots), grid=(2 * t...  25.9 us
    pallas_call x1, Pallas kernels, fetch_call(): pl.pallas_call(functools.partial(fetch_kernel, bands, sectors), in_specs=...  12.9 us
    pallas_call x1, Pallas kernels, close_call(): pl.pallas_call(functools.partial(close_kernel, scale), in_specs=[whole, t...  3.67 us

profile of v6, /device:TPU:1, one launch (start us, length us, event | category | flops | bytes accessed | tf_op | source)
XLA Modules:
  0.0 74.8 jit_solution(3815355205310541594)
XLA Ops:
  0.6 12.9 %shard_map.206 = bf16[8,64,256]{2,1,0:T(8,128)(2,1)} custom-call(bf16[512,256]{1,0:T(8,128)(2,1)} %own_ref.1, s32[1,8,64]{2,1,0:T(8,128)} %rows_ref.3), custom_call_target="tpu_custom_call" | custom-call | tf_op jit(solution)/shard_map/pallas_call | solution.py:385
  13.5 25.9 %shard_map.207 = (bf16[512,256]{1,0:T(8,128)(2,1)}, bf16[6144,256]{1,0:T(8,128)(2,1)}, bf16[6144,256]{1,0:T(8,128)(2,1)}, f32[512,256]{1,0:T(8,128)}, bf16[8,64,...) custom-call(bf16[512,256]{1,0:T(8,128)(2,1)} %own_ref.1, bf16[512,256]{1,0:T(8,128)(2,1)} %bitcast.11, ...), custom_call_target="tpu_custom_call" | custom-call | flops 12884901888 | bytes 15728640 | tf_op jit(solution)/shard_map/pallas_call | solution.py:276
  39.5 31.7 %shard_map.208 = (bf16[8,64,256]{2,1,0:T(8,128)(2,1)}, bf16[2,112,16,128]{3,2,1,0:T(8,128)(2,1)}) custom-call(bf16[8,64,256]{2,1,0:T(8,128)(2,1)} %get-tuple-element.23.back_ref, bf16[2,112,16,128]{3,2,1,0:T(8,128)(2,1)} %bitcast.9), custom_call_target="tpu_custom_call" | custom-call | tf_op jit(solution)/shard_map/pallas_call | solution.py:553
  71.2 3.7 %shard_map.209 = (f32[512,256]{1,0:T(8,128)}, f32[768,256]{1,0:T(8,128)}, f32[256,256]{1,0:T(8,128)}, f32[512,256]{1,0:T(8,128)}, f32[256,256]{1,0:T(8,128)}) custom-call(s32[1,8,64]{2,1,0:T(8,128)} %rows_ref.3, bf16[8,64,256]{2,1,0:T(8,128)(2,1)} %get-tuple-element.25.arrived_hbm, f32[512,256]{1,0:T(8,128)} %get-tuple-element.26.part_hbm, ...), custom_call_target="tpu_custom_call" | custom-call | tf_op jit(solution)/shard_map/pallas_call | solution.py:628
